TPU v7x, 32 devices: a whole 2x2x4 slice. The times are simulated.
32 devices in a mesh: depth: 4 (over z), row: 4 (over y, x), col: 2 (over core).
Axes of the slice: x: 2, y: 2, z: 4, core: 2. Of those that a mesh axis runs over, the one named last changes fastest.
Arguments:
- density: bfloat16 [32, 512, 512], P('depth', 'row', 'col'), may hold values from 0.009338379 to 0.1875
- emission: bfloat16 [3, 32, 512, 512], P(None, 'depth', 'row', 'col'), may hold values from 0.19921875 to 5
- offsets: int32 [3, 2, 4, 4, 4], P(None, None, 'depth', 'row', 'col'), may hold values from -8 to 8
- view_order: int32 [3, 4], P(None, 'row'), may hold values from 0 to 1
Outputs:
- image: float32 [3, 4, 128, 4, 512], P(None, None, 'row', 'depth', 'col')
Inputs may be any that keep to these rules, and one draw needn't show every extreme that they name: `offsets`: displacement in cells of each brick's footprint from its home position in each view. `view_order`: 1 reverses the rays' direction along depth in that view and band of brick rows.
All inputs are finite; a program needn't handle non-finite values.
Results may differ from a plain program's by a relative error of at most 0.00052.
Values sent between devices are 32-bit elements; how exact they have to be, the bound alone decides.
No kernel may reach another device: no remote copies, remote signals or barrier semaphores. Data moves between devices by JAX's collectives and lax.ppermute only.
A program may use at most 128 MiB of HBM per device.

v0:
```python
import jax
import jax.numpy as jnp
from jax import lax
from jax.sharding import PartitionSpec as P

MARGIN = 16
JIT = 8
VIEWS = 3


SHEAR_ROWS = (0.75, -0.5, 0.25)
SHEAR_COLS = (-0.25, 0.625, -0.875)


def partner(block, axis, stride):
    count = lax.axis_size(axis)
    route = []
    for low in range(count):
        high = low | 1 << stride
        if high != low and high < count:
            route += [(low, high), (high, low)]
    return lax.ppermute(block, axis, route)


def extended(block, sides, width):
    for axis, dim in sides:
        count = lax.axis_size(axis)
        forward = [(i, i + 1) for i in range(count - 1)]
        forward.append((count - 1, 0))
        backward = [(target, source) for source, target in forward]
        low = lax.ppermute(
            lax.slice_in_dim(block, block.shape[dim] - width, None, axis=dim), axis, forward
        )
        high = lax.ppermute(lax.slice_in_dim(block, 0, width, axis=dim), axis, backward)
        block = jnp.concatenate([low, block, high], axis=dim)
    return block


def bilinear(shear_rate, slices, length, margin):
    tile_width = length + 2 * margin
    slice_pos = jnp.arange(slices, dtype=jnp.float32)
    slice_shift = shear_rate * (margin - 2) * (2.0 * slice_pos - (slices - 1)) / slices
    target = jnp.arange(tile_width, dtype=jnp.float32)
    source = jnp.arange(length, dtype=jnp.float32)
    distance = target[None, :, None] - margin - slice_shift[:, None, None] - source[None, None, :]
    return jnp.maximum(0.0, 1.0 - jnp.abs(distance)).astype(jnp.bfloat16)


def integrate(footprint, backward):
    extinction = footprint[0]
    running = jnp.cumsum(extinction, axis=-3)
    total_depth = jnp.sum(extinction, axis=-3)
    prefix_depth = jnp.where(backward, total_depth[..., None, :, :] - running, running - extinction)
    weight = (1.0 - jnp.exp(-extinction)) * jnp.exp(-prefix_depth)
    colors = jnp.sum(footprint[1:] * weight, axis=-3)
    return jnp.concatenate([colors, total_depth[None]], 0)


def pad_along(source_array, lead_count, trail_count, axis_pos):
    widths = [(0, 0)] * source_array.ndim
    widths[axis_pos] = (lead_count, trail_count)
    return jnp.pad(source_array, widths)


def fold_rims(padded, rim_width, cell_count, axis_pos):
    interior = lax.slice_in_dim(padded, 2 * rim_width, 2 * rim_width + cell_count, axis=axis_pos)
    from_above = lax.slice_in_dim(padded, 0, rim_width, axis=axis_pos)
    from_below = lax.slice_in_dim(
        padded, cell_count + 3 * rim_width, cell_count + 4 * rim_width, axis=axis_pos
    )
    return (
        interior
        + pad_along(from_above, 0, cell_count - rim_width, axis_pos)
        + pad_along(from_below, cell_count - rim_width, 0, axis_pos)
    )


def render_view(fields, view_index, offsets, backward):
    slices = fields.shape[1]
    length = fields.shape[2]
    bricks = fields.shape[3]
    row_weights = bilinear(SHEAR_ROWS[view_index], slices, length, MARGIN)
    col_weights = bilinear(SHEAR_COLS[view_index], slices, length, MARGIN)
    resampled = jnp.einsum(
        "fzybx,zux->fzybu", fields, col_weights, preferred_element_type=jnp.float32
    ).astype(jnp.bfloat16)
    footprint = jnp.einsum(
        "zty,fzybu->fbztu", row_weights, resampled, preferred_element_type=jnp.float32
    )
    shaded = integrate(footprint, backward)
    rim_width = MARGIN + JIT
    tile_width = length + 2 * MARGIN
    canvas = jnp.zeros((4, length + 2 * rim_width, bricks * length + 2 * rim_width), jnp.float32)
    for brick_index in range(bricks):
        top_row = offsets[view_index, 0, 0, 0, brick_index] + JIT
        left_col = offsets[view_index, 1, 0, 0, brick_index] + brick_index * length + JIT
        corner = (jnp.int32(0), top_row, left_col)
        current = lax.dynamic_slice(canvas, corner, (4, tile_width, tile_width))
        canvas = lax.dynamic_update_slice(canvas, current + shaded[:, brick_index], corner)
    return canvas


def over_combine(front_part, back_part):
    screen = jnp.exp(-front_part[:, 3:4])
    colors = front_part[:, :3] + screen * back_part[:, :3]
    return jnp.concatenate([colors, front_part[:, 3:4] + back_part[:, 3:4]], 1)


def composite(owned, orders):
    view_count, channels, length, columns = owned.shape
    sections = lax.axis_size("depth")
    phase_rows = length // sections
    backward = (orders == 1)[:, None, None, None, None]
    current = owned.reshape(view_count, channels, phase_rows, sections, columns)
    position = lax.axis_index("depth")
    for section_bit in range(sections.bit_length() - 1):
        paired = current.reshape(
            view_count, channels, phase_rows, current.shape[3] // 2, 2, columns
        )
        mine_bit = position >> section_bit & 1
        lower_half = paired[:, :, :, :, 0]
        upper_half = paired[:, :, :, :, 1]
        kept_half = jnp.where(mine_bit == 0, lower_half, upper_half)
        given_half = jnp.where(mine_bit == 0, upper_half, lower_half)
        received = partner(given_half, "depth", section_bit)
        mine_front = jnp.logical_xor(mine_bit == 0, backward)
        front_part = jnp.where(mine_front, kept_half, received)
        back_part = jnp.where(mine_front, received, kept_half)
        current = over_combine(front_part, back_part)
    colors = current[:, :3]
    depth_sum = current[:, 3:4]
    return jnp.concatenate([colors, jnp.exp(-depth_sum)], 1)


def spill_and_composite(canvases, orders, length, columns):
    rim_width = MARGIN + JIT
    padded = extended(canvases, (("row", 2), ("col", 3)), rim_width)
    owned = fold_rims(fold_rims(padded, rim_width, length, 2), rim_width, columns, 3)
    return composite(owned, orders)


def local(density, emission, offsets, view_order):
    slices, length, columns = density.shape
    bricks = columns // length
    band_orders = view_order[:, 0]
    fields = jnp.concatenate([density[None], emission], 0).reshape(
        4, slices, length, bricks, length
    )
    per_view = []
    for view_index in range(VIEWS):
        canvas = render_view(fields, view_index, offsets, band_orders[view_index] == 1)
        per_view.append(
            spill_and_composite(
                canvas[None], band_orders[view_index : view_index + 1], length, columns
            )
        )
    return jnp.concatenate(per_view, 0)


def solution(mesh):
    return jax.shard_map(
        local,
        mesh=mesh,
        in_specs=(
            P("depth", "row", "col"),
            P(None, "depth", "row", "col"),
            P(None, None, "depth", "row", "col"),
            P(None, "row"),
        ),
        out_specs=P(None, None, "row", "depth", "col"),
        check_vma=False,
    )
```

profile of v0, /device:TPU:0, one launch (start us, length us, event | category | flops | bytes accessed | tf_op | source)
XLA Modules:
  0.0 202.7 jit_solution(151497409335062119)
XLA Ops:
  0.1 2.6 %copy.95 = bf16[3,8,128,256]{2,3,1,0:T(8,128)(2,1)} copy(bf16[3,8,128,256]{3,2,1,0:T(8,128)(2,1)} %param.5) | data formatting | bytes 3145728 | tf_op args[1]
  2.7 1.9 copy.97
  5.3 5.3 %convolution_bitcast_fusion = f32[4,2,8,160,160]{3,4,1,0,2:T(8,128)} fusion(bf16[3,8,128,2,128]{4,2,3,0,1:T(8,128)(2,1)S(1)} %copy.97, bf16[1,8,128,2,128]{4,2,3,0,1:T(8,128)(2,1)S(1)} %copy.96, f32[8,160]{1,0:T(8,128)S(1)} %get-tuple-element.65, f32[8,160]{1,0:T(8,128)S(1)} %get-tuple-element.64), kind=kOutput, calls=%fused_computation.6 | convolution fusion | flops 762118144 | bytes 8660992 | tf_op jit(solution)/shard_map/zty,fzybu->fbztu/dot_general | solution.py:87
  10.6 2.0 slice_reduce_fusion
  12.6 2.1 %fusion.15 = f32[1,2,8,160,160]{3,4,1,0,2:T(8,128)S(1)} fusion(f32[4,2,8,160,160]{3,4,1,0,2:T(8,128)} %convolution_bitcast_fusion), kind=kOutput, calls=%fused_computation.21 | output fusion | flops 2867200 | bytes 4259840 | tf_op jit(solution)/shard_map/jit(cumsum)/reduce_window_sum | solution.py:51
  19.9 2.5 %multiply_bitcast_fusion = f32[2,8,160,160]{2,3,0,1:T(8,128)S(1)} fusion(f32[1,2,8,160,160]{3,4,1,0,2:T(8,128)S(1)} %fusion.15, f32[4,2,8,160,160]{3,4,1,0,2:T(8,128)} %convolution_bitcast_fusion, f32[2,160,160]{1,2,0:T(8,128)S(1)} %slice_reduce_fusion, pred[]{:T(512)} %bitcast.77), kind=kLoop, calls=%fused_computation.12 | loop fusion | flops 2867200 | bytes 5120001 | tf_op jit(solution)/shard_map/mul | solution.py:55
  26.2 1.8 fusion.28
  28.1 7.5 %dynamic_update_slice.25 = f32[4,176,304]{1,2,0:T(8,128)S(1)} dynamic-update-slice(f32[4,176,304]{1,2,0:T(8,128)S(1)} %broadcast.434.clone.2, f32[4,160,160]{1,2,0:T(8,128)} %fusion.28, s32[]{:T(128)} %constant.102.clone.1, s32[]{:T(128)S(6)} %select_n.331, s32[]{:T(128)S(6)} %select_n.332) | dynamic-update-slice | bytes 819204 | tf_op jit(solution)/shard_map/dynamic_update_slice | solution.py:99
  35.6 2.2 %fusion.35 = f32[1,4,160,160]{2,3,1,0:T(8,128)} fusion(f32[1,2,160,160]{2,3,0,1:T(8,128)} %bitcast.218, f32[4,176,304]{1,2,0:T(8,128)S(1)} %dynamic_update_slice.25, s32[]{:T(128)S(6)} %select_n.333, s32[]{:T(128)S(6)} %select_n.334, f32[3,2,160,160]{2,3,1,0:T(8,128)} %copy-done.6), kind=kLoop, calls=%fused_computation.58 | loop fusion | flops 204800 | bytes 1638408 | tf_op jit(solution)/shard_map/broadcast_in_dim | solution.py:154
  37.9 6.7 %dynamic_update_slice.26 = f32[1,4,176,304]{2,3,1,0:T(8,128)S(1)} dynamic-update-slice(f32[1,4,176,304]{2,3,1,0:T(8,128)S(1)} %bitcast.214, f32[1,4,160,160]{2,3,1,0:T(8,128)} %fusion.35, s32[]{:T(128)} %constant.102.clone.1, s32[]{:T(128)} %constant.102.clone.1, s32[]{:T(128)S(6)} %select_n.333, s32[]{:T(128)S(6)} %select_n.334) | dynamic-update-slice | bytes 819204 | tf_op jit(solution)/shard_map/dynamic_update_slice | solution.py:99
  45.8 2.0 copy.125
  47.8 2.9 %collective-permute-start.12 = (f32[1,4,24,304]{3,2,1,0:T(8,128)}, f32[1,4,24,304]{3,2,1,0:T(8,128)}, u32[]{:S(2)}, u32[]{:S(2)}) collective-permute-start(f32[1,4,24,304]{3,2,1,0:T(8,128)} %copy.125), channel_id=1, source_target_pairs={{0,2},{2,4},{4,6},{6,0},{1,3},{3,5},{5,7},{7,1},{8,10},{10,12},{12... | collective-permute-start | bytes 350216 | tf_op jit(solution)/shard_map/ppermute | solution.py:31
  50.7 2.0 copy.126
  53.7 5.3 %convolution_bitcast_fusion.1 = f32[4,2,8,160,160]{3,4,1,0,2:T(8,128)} fusion(bf16[3,8,128,2,128]{4,2,3,0,1:T(8,128)(2,1)S(1)} %copy.97, bf16[1,8,128,2,128]{4,2,3,0,1:T(8,128)(2,1)S(1)} %copy.96, f32[8,160]{1,0:T(8,128)S(1)} %get-tuple-element.63, f32[8,160]{1,0:T(8,128)S(1)} %get-tuple-element.62), kind=kOutput, calls=%fused_computation.7 | convolution fusion | flops 762118144 | bytes 8660992 | tf_op jit(solution)/shard_map/zty,fzybu->fbztu/dot_general | solution.py:87
  59.0 2.0 slice_reduce_fusion.1
  60.9 2.1 %fusion.17 = f32[1,2,8,160,160]{3,4,1,0,2:T(8,128)S(1)} fusion(f32[4,2,8,160,160]{3,4,1,0,2:T(8,128)} %convolution_bitcast_fusion.1), kind=kOutput, calls=%fused_computation.24 | output fusion | flops 2867200 | bytes 4259840 | tf_op jit(solution)/shard_map/jit(cumsum)/reduce_window_sum | solution.py:51
  69.6 2.5 %multiply_bitcast_fusion.1 = f32[2,8,160,160]{2,3,0,1:T(8,128)S(1)} fusion(f32[1,2,8,160,160]{3,4,1,0,2:T(8,128)S(1)} %fusion.17, f32[4,2,8,160,160]{3,4,1,0,2:T(8,128)} %convolution_bitcast_fusion.1, f32[2,160,160]{1,2,0:T(8,128)S(1)} %slice_reduce_fusion.1, pred[]{:T(512)} %bitcast.47), kind=kLoop, calls=%fused_computation.14 | loop fusion | flops 2867200 | bytes 5120001 | tf_op jit(solution)/shard_map/mul | solution.py:55
  74.3 7.6 %dynamic_update_slice.23 = f32[4,176,304]{1,2,0:T(8,128)S(1)} dynamic-update-slice(f32[4,176,304]{1,2,0:T(8,128)S(1)} %broadcast.434.clone.1, f32[4,160,160]{1,2,0:T(8,128)} %fusion.30, s32[]{:T(128)} %constant.102.clone.1, s32[]{:T(128)S(6)} %select_n.313, s32[]{:T(128)S(6)} %select_n.314) | dynamic-update-slice | bytes 819204 | tf_op jit(solution)/shard_map/dynamic_update_slice | solution.py:99
  81.8 2.0 fusion.38
  83.8 6.6 %dynamic_update_slice.24 = f32[1,4,176,304]{2,3,1,0:T(8,128)S(1)} dynamic-update-slice(f32[1,4,176,304]{2,3,1,0:T(8,128)S(1)} %bitcast.215, f32[1,4,160,160]{2,3,1,0:T(8,128)} %fusion.38, s32[]{:T(128)} %constant.102.clone.1, s32[]{:T(128)} %constant.102.clone.1, s32[]{:T(128)S(6)} %select_n.315, s32[]{:T(128)S(6)} %select_n.316) | dynamic-update-slice | bytes 819204 | tf_op jit(solution)/shard_map/dynamic_update_slice | solution.py:99
  90.5 1.5 fusion.117
  92.0 2.0 copy.116
  95.0 2.0 copy.117
  96.9 1.9 collective-permute-start.7
  98.8 7.7 %convolution_bitcast_fusion.2 = f32[4,2,8,160,160]{3,4,1,0,2:T(8,128)} fusion(bf16[3,8,128,2,128]{4,2,3,0,1:T(8,128)(2,1)} %copy-done.5, bf16[1,8,128,2,128]{4,2,3,0,1:T(8,128)(2,1)S(1)} %copy-done.8, f32[8,160]{1,0:T(8,128)S(1)} %get-tuple-element.61, f32[8,160]{1,0:T(8,128)S(1)} %get-tuple-element.60), kind=kOutput, calls=%fused_computation.8 | convolution fusion | flops 762118144 | bytes 8660992 | tf_op jit(solution)/shard_map/zty,fzybu->fbztu/dot_general | solution.py:87
  106.5 2.0 slice_reduce_fusion.2
  108.5 2.1 %fusion.19 = f32[1,2,8,160,160]{3,4,1,0,2:T(8,128)S(1)} fusion(f32[4,2,8,160,160]{3,4,1,0,2:T(8,128)} %convolution_bitcast_fusion.2), kind=kOutput, calls=%fused_computation.27 | output fusion | flops 2867200 | bytes 4259840 | tf_op jit(solution)/shard_map/jit(cumsum)/reduce_window_sum | solution.py:51
  117.0 2.5 %multiply_bitcast_fusion.2 = f32[2,8,160,160]{2,3,0,1:T(8,128)S(1)} fusion(f32[1,2,8,160,160]{3,4,1,0,2:T(8,128)S(1)} %fusion.19, f32[4,2,8,160,160]{3,4,1,0,2:T(8,128)} %convolution_bitcast_fusion.2, f32[2,160,160]{1,2,0:T(8,128)S(1)} %slice_reduce_fusion.2, pred[]{:T(512)} %bitcast.14), kind=kLoop, calls=%fused_computation.16 | loop fusion | flops 2867200 | bytes 5120001 | tf_op jit(solution)/shard_map/mul | solution.py:55
  121.7 7.5 %dynamic_update_slice.21 = f32[4,176,304]{1,2,0:T(8,128)S(1)} dynamic-update-slice(f32[4,176,304]{1,2,0:T(8,128)S(1)} %broadcast.434.clone, f32[4,160,160]{1,2,0:T(8,128)} %fusion.32, s32[]{:T(128)} %constant.102.clone.1, s32[]{:T(128)S(6)} %select_n.295, s32[]{:T(128)S(6)} %select_n.296) | dynamic-update-slice | bytes 819204 | tf_op jit(solution)/shard_map/dynamic_update_slice | solution.py:99
  129.2 2.0 fusion.41
  131.2 6.5 %dynamic_update_slice.22 = f32[1,4,176,304]{2,3,1,0:T(8,128)S(1)} dynamic-update-slice(f32[1,4,176,304]{2,3,1,0:T(8,128)S(1)} %bitcast.213, f32[1,4,160,160]{2,3,1,0:T(8,128)} %fusion.41, s32[]{:T(128)} %constant.102.clone.1, s32[]{:T(128)} %constant.102.clone.1, s32[]{:T(128)S(6)} %select_n.297, s32[]{:T(128)S(6)} %select_n.298) | dynamic-update-slice | bytes 819204 | tf_op jit(solution)/shard_map/dynamic_update_slice | solution.py:99
  138.8 1.3 copy.99
  140.4 3.2 %collective-permute-start.1 = (f32[1,4,24,304]{3,2,1,0:T(8,128)S(1)}, f32[1,4,24,304]{3,2,1,0:T(8,128)}, u32[]{:S(2)}, u32[]{:S(2)}) collective-permute-start(f32[1,4,24,304]{3,2,1,0:T(8,128)S(1)} %copy.100), channel_id=1, source_target_pairs={{2,0},{4,2},{6,4},{0,6},{3,1},{5,3},{7,5},{1,7},{10,8},{12,10},{14... | collective-permute-start | bytes 350216 | tf_op jit(solution)/shard_map/ppermute | solution.py:34
  144.7 2.0 copy.128
  146.7 1.6 pad_maximum_fusion.15
  148.9 2.0 copy.118
  150.9 2.0 copy.119
  152.8 1.8 pad_maximum_fusion.18
  156.2 2.0 copy.102
  159.9 1.7 pad_maximum_fusion.3
  162.0 1.5 pad_maximum_fusion.2
  170.6 5.2 %collective-permute-done.4 = f32[1,4,32,2,256]{4,1,3,2,0:T(4,128)S(1)} collective-permute-done((f32[1,4,32,2,256]{4,1,3,2,0:T(4,128)S(1)}, f32[1,4,32,2,256]{4,1,3,2,0:T(4,128)S(1)}, u32[]{:S(2)}, u32[]{:S(2)}) %collective-permute-start.4) | collective-permute-done | bytes 262176 | tf_op jit(solution)/shard_map/ppermute | solution.py:22
  176.4 3.1 %collective-permute-start.5 = (f32[1,4,32,1,256]{4,1,2,3,0:T(4,128)S(1)}, f32[1,4,32,1,256]{4,1,2,3,0:T(4,128)S(1)}, u32[]{:S(2)}, u32[]{:S(2)}) collective-permute-start(f32[1,4,32,1,256]{4,1,2,3,0:T(4,128)S(1)} %select_bitcast_fusion.5), channel_id=1, source_target_pairs={{0,16},{16,0},{8,24},{24,8},{1,17},{17,1},{9,25},{25,9},{2,18},{18... | collective-permute-start | bytes 393224 | tf_op jit(solution)/shard_map/ppermute | solution.py:22
  179.6 4.7 %collective-permute-done.10 = f32[1,4,32,2,256]{4,1,2,3,0:T(4,128)S(1)} collective-permute-done((f32[1,4,32,2,256]{4,1,2,3,0:T(4,128)S(1)}, f32[1,4,32,2,256]{4,1,2,3,0:T(4,128)S(1)}, u32[]{:S(2)}, u32[]{:S(2)}) %collective-permute-start.10) | collective-permute-done | bytes 262176 | tf_op jit(solution)/shard_map/ppermute | solution.py:22
  184.8 2.3 %collective-permute-start.11 = (f32[1,4,32,1,256]{4,1,2,3,0:T(4,128)S(1)}, f32[1,4,32,1,256]{4,1,2,3,0:T(4,128)S(1)}, u32[]{:S(2)}, u32[]{:S(2)}) collective-permute-start(f32[1,4,32,1,256]{4,1,2,3,0:T(4,128)S(1)} %select_bitcast_fusion.4), channel_id=1, source_target_pairs={{0,16},{16,0},{8,24},{24,8},{1,17},{17,1},{9,25},{25,9},{2,18},{18... | collective-permute-start | bytes 393224 | tf_op jit(solution)/shard_map/ppermute | solution.py:22
  187.1 3.4 %collective-permute-done.16 = f32[1,4,32,2,256]{4,1,2,3,0:T(4,128)S(1)} collective-permute-done((f32[1,4,32,2,256]{4,1,2,3,0:T(4,128)S(1)}, f32[1,4,32,2,256]{4,1,2,3,0:T(4,128)S(1)}, u32[]{:S(2)}, u32[]{:S(2)}) %collective-permute-start.16) | collective-permute-done | bytes 262176 | tf_op jit(solution)/shard_map/ppermute | solution.py:22
  192.4 7.1 %collective-permute-done.11 = f32[1,4,32,1,256]{4,1,2,3,0:T(4,128)S(1)} collective-permute-done((f32[1,4,32,1,256]{4,1,2,3,0:T(4,128)S(1)}, f32[1,4,32,1,256]{4,1,2,3,0:T(4,128)S(1)}, u32[]{:S(2)}, u32[]{:S(2)}) %collective-permute-start.11) | collective-permute-done | bytes 131104 | tf_op jit(solution)/shard_map/ppermute | solution.py:22
  199.7 1.4 collective-permute-done.17
  (144 shorter events, 29.2 us)
Async XLA Ops:
  0.0 4.6 %copy-start.18 = (bf16[8,128,256]{2,1,0:T(8,128)(2,1)S(1)}, bf16[8,128,256]{2,1,0:T(8,128)(2,1)}, u32[]{:S(2)}) copy-start(bf16[8,128,256]{2,1,0:T(8,128)(2,1)} %param.4) | copy-start | bytes 1572868
  4.6 49.1 %copy-start.5 = (bf16[3,8,128,2,128]{4,2,3,0,1:T(8,128)(2,1)}, bf16[3,8,128,2,128]{4,2,3,0,1:T(8,128)(2,1)S(1)}, u32[]{:S(2)}) copy-start(bf16[3,8,128,2,128]{4,2,3,0,1:T(8,128)(2,1)S(1)} %copy.97) | copy-start | bytes 4718596
  5.2 48.5 %copy-start.7 = (bf16[1,8,128,2,128]{4,2,3,0,1:T(8,128)(2,1)}, bf16[1,8,128,2,128]{4,2,3,0,1:T(8,128)(2,1)S(1)}, u32[]{:S(2)}) copy-start(bf16[1,8,128,2,128]{4,2,3,0,1:T(8,128)(2,1)S(1)} %copy.96) | copy-start | bytes 1572868
  10.6 4.1 %copy-start.19 = (s32[3,2,1,1,2]{0,4,3,2,1:T(2,128)S(1)}, s32[3,2,1,1,2]{0,4,3,2,1:T(2,128)}, u32[]{:S(2)}) copy-start(s32[3,2,1,1,2]{0,4,3,2,1:T(2,128)} %param.6) | copy-start | bytes 148
  10.6 7.9 %copy-start.20 = (s32[3,1]{0,1:T(1,128)S(1)}, s32[3,1]{0,1:T(1,128)}, u32[]{:S(2)}) copy-start(s32[3,1]{0,1:T(1,128)} %param.7) | copy-start | bytes 40
  12.5 7.3 %copy-start.14 = (f32[2,160,160]{1,2,0:T(8,128)}, f32[2,160,160]{1,2,0:T(8,128)S(1)}, u32[]{:S(2)}) copy-start(f32[2,160,160]{1,2,0:T(8,128)S(1)} %slice_reduce_fusion) | copy-start | bytes 614404
  12.6 9.8 %copy-start = (f32[4,2,8,160,160]{3,4,1,0,2:T(8,128)S(1)}, f32[4,2,8,160,160]{3,4,1,0,2:T(8,128)}, u32[]{:S(2)}) copy-start(f32[4,2,8,160,160]{3,4,1,0,2:T(8,128)} %convolution_bitcast_fusion) | copy-start | bytes 19660804
  23.6 4.5 %copy-start.6 = (f32[3,2,160,160]{2,3,1,0:T(8,128)}, f32[3,2,160,160]{2,3,1,0:T(8,128)S(1)}, u32[]{:S(2)}) copy-start(f32[3,2,160,160]{2,3,1,0:T(8,128)S(1)} %fusion) | copy-start | bytes 1843204
  47.8 92.6 %collective-permute-start.12 = (f32[1,4,24,304]{3,2,1,0:T(8,128)}, f32[1,4,24,304]{3,2,1,0:T(8,128)}, u32[]{:S(2)}, u32[]{:S(2)}) collective-permute-start(f32[1,4,24,304]{3,2,1,0:T(8,128)} %copy.125), channel_id=1, source_target_pairs={{0,2},{2,4},{4,6},{6,0},{1,3},{3,5},{5,7},{7,1},{8,10},{10,12},{12... | collective-permute-start | bytes 350216 | tf_op jit(solution)/shard_map/ppermute | solution.py:31
  52.7 92.0 %collective-permute-start.13 = (f32[1,4,24,304]{3,2,1,0:T(8,128)}, f32[1,4,24,304]{3,2,1,0:T(8,128)}, u32[]{:S(2)}, u32[]{:S(2)}) collective-permute-start(f32[1,4,24,304]{3,2,1,0:T(8,128)} %copy.126), channel_id=1, source_target_pairs={{2,0},{4,2},{6,4},{0,6},{3,1},{5,3},{7,5},{1,7},{10,8},{12,10},{14... | collective-permute-start | bytes 350216 | tf_op jit(solution)/shard_map/ppermute | solution.py:34
  60.9 12.4 %copy-start.17 = (f32[2,160,160]{1,2,0:T(8,128)}, f32[2,160,160]{1,2,0:T(8,128)S(1)}, u32[]{:S(2)}) copy-start(f32[2,160,160]{1,2,0:T(8,128)S(1)} %slice_reduce_fusion.1) | copy-start | bytes 614404
  60.9 11.1 %copy-start.2 = (f32[4,2,8,160,160]{3,4,1,0,2:T(8,128)S(1)}, f32[4,2,8,160,160]{3,4,1,0,2:T(8,128)}, u32[]{:S(2)}) copy-start(f32[4,2,8,160,160]{3,4,1,0,2:T(8,128)} %convolution_bitcast_fusion.1) | copy-start | bytes 19660804
  83.8 15.0 %copy-start.8 = (bf16[1,8,128,2,128]{4,2,3,0,1:T(8,128)(2,1)S(1)}, bf16[1,8,128,2,128]{4,2,3,0,1:T(8,128)(2,1)}, u32[]{:S(2)}) copy-start(bf16[1,8,128,2,128]{4,2,3,0,1:T(8,128)(2,1)} %copy-done.7) | copy-start | bytes 1572868
  90.5 16.0 %copy-start.3 = (f32[1,4,176,304]{2,3,1,0:T(8,128)}, f32[1,4,176,304]{2,3,1,0:T(8,128)S(1)}, u32[]{:S(2)}) copy-start(f32[1,4,176,304]{2,3,1,0:T(8,128)S(1)} %dynamic_update_slice.24) | copy-start | bytes 2568196
  93.9 54.4 %collective-permute-start.6 = (f32[1,4,24,304]{3,2,1,0:T(8,128)}, f32[1,4,24,304]{3,2,1,0:T(8,128)}, u32[]{:S(2)}, u32[]{:S(2)}) collective-permute-start(f32[1,4,24,304]{3,2,1,0:T(8,128)} %copy.116), channel_id=1, source_target_pairs={{0,2},{2,4},{4,6},{6,0},{1,3},{3,5},{5,7},{7,1},{8,10},{10,12},{12... | collective-permute-start | bytes 350216 | tf_op jit(solution)/shard_map/ppermute | solution.py:31
  96.9 53.9 %collective-permute-start.7 = (f32[1,4,24,304]{3,2,1,0:T(8,128)}, f32[1,4,24,304]{3,2,1,0:T(8,128)}, u32[]{:S(2)}, u32[]{:S(2)}) collective-permute-start(f32[1,4,24,304]{3,2,1,0:T(8,128)} %copy.117), channel_id=1, source_target_pairs={{2,0},{4,2},{6,4},{0,6},{3,1},{5,3},{7,5},{1,7},{10,8},{12,10},{14... | collective-permute-start | bytes 350216 | tf_op jit(solution)/shard_map/ppermute | solution.py:34
  108.5 8.5 %copy-start.15 = (f32[2,160,160]{1,2,0:T(8,128)}, f32[2,160,160]{1,2,0:T(8,128)S(1)}, u32[]{:S(2)}) copy-start(f32[2,160,160]{1,2,0:T(8,128)S(1)} %slice_reduce_fusion.2) | copy-start | bytes 614404
  108.5 11.0 %copy-start.1 = (f32[4,2,8,160,160]{3,4,1,0,2:T(8,128)S(1)}, f32[4,2,8,160,160]{3,4,1,0,2:T(8,128)}, u32[]{:S(2)}) copy-start(f32[4,2,8,160,160]{3,4,1,0,2:T(8,128)} %convolution_bitcast_fusion.2) | copy-start | bytes 19660804
  119.5 1.2 copy-start.16
  140.1 14.6 %collective-permute-start = (f32[1,4,24,304]{3,2,1,0:T(8,128)S(1)}, f32[1,4,24,304]{3,2,1,0:T(8,128)S(1)}, u32[]{:S(2)}, u32[]{:S(2)}) collective-permute-start(f32[1,4,24,304]{3,2,1,0:T(8,128)S(1)} %copy.99), channel_id=1, source_target_pairs={{0,2},{2,4},{4,6},{6,0},{1,3},{3,5},{5,7},{7,1},{8,10},{10,12},{12... | collective-permute-start | bytes 350216 | tf_op jit(solution)/shard_map/ppermute | solution.py:31
  140.4 15.8 %collective-permute-start.1 = (f32[1,4,24,304]{3,2,1,0:T(8,128)S(1)}, f32[1,4,24,304]{3,2,1,0:T(8,128)}, u32[]{:S(2)}, u32[]{:S(2)}) collective-permute-start(f32[1,4,24,304]{3,2,1,0:T(8,128)S(1)} %copy.100), channel_id=1, source_target_pairs={{2,0},{4,2},{6,4},{0,6},{3,1},{5,3},{7,5},{1,7},{10,8},{12,10},{14... | collective-permute-start | bytes 350216 | tf_op jit(solution)/shard_map/ppermute | solution.py:34
  148.3 11.1 %collective-permute-start.14 = (f32[1,4,224,24]{2,3,1,0:T(8,128)}, f32[1,4,224,24]{2,3,1,0:T(8,128)}, u32[]{:S(2)}, u32[]{:S(2)}) collective-permute-start(f32[1,4,224,24]{2,3,1,0:T(8,128)} %get-tuple-element.9), channel_id=1, source_target_pairs={{0,1},{1,0},{2,3},{3,2},{4,5},{5,4},{6,7},{7,6},{8,9},{9,8},{10,11... | collective-permute-start | bytes 258056 | tf_op jit(solution)/shard_map/ppermute | solution.py:31
  148.3 11.6 %collective-permute-start.15 = (f32[1,4,224,24]{2,3,1,0:T(8,128)}, f32[1,4,224,24]{2,3,1,0:T(8,128)}, u32[]{:S(2)}, u32[]{:S(2)}) collective-permute-start(f32[1,4,224,24]{2,3,1,0:T(8,128)} %get-tuple-element.10), channel_id=1, source_target_pairs={{1,0},{0,1},{3,2},{2,3},{5,4},{4,5},{7,6},{6,7},{9,8},{8,9},{11,10... | collective-permute-start | bytes 258056 | tf_op jit(solution)/shard_map/ppermute | solution.py:34
  154.6 7.3 %collective-permute-start.8 = (f32[1,4,224,24]{2,3,1,0:T(8,128)}, f32[1,4,224,24]{2,3,1,0:T(8,128)}, u32[]{:S(2)}, u32[]{:S(2)}) collective-permute-start(f32[1,4,224,24]{2,3,1,0:T(8,128)} %get-tuple-element.7), channel_id=1, source_target_pairs={{0,1},{1,0},{2,3},{3,2},{4,5},{5,4},{6,7},{7,6},{8,9},{9,8},{10,11... | collective-permute-start | bytes 258056 | tf_op jit(solution)/shard_map/ppermute | solution.py:31
  154.7 7.3 %collective-permute-start.9 = (f32[1,4,224,24]{2,3,1,0:T(8,128)}, f32[1,4,224,24]{2,3,1,0:T(8,128)S(1)}, u32[]{:S(2)}, u32[]{:S(2)}) collective-permute-start(f32[1,4,224,24]{2,3,1,0:T(8,128)} %get-tuple-element.8), channel_id=1, source_target_pairs={{1,0},{0,1},{3,2},{2,3},{5,4},{4,5},{7,6},{6,7},{9,8},{8,9},{11,10... | collective-permute-start | bytes 258056 | tf_op jit(solution)/shard_map/ppermute | solution.py:34
  158.2 1.7 copy-start.9
  159.3 4.5 %collective-permute-start.2 = (f32[1,4,224,24]{2,3,1,0:T(8,128)S(1)}, f32[1,4,224,24]{2,3,1,0:T(8,128)S(1)}, u32[]{:S(2)}, u32[]{:S(2)}) collective-permute-start(f32[1,4,224,24]{2,3,1,0:T(8,128)S(1)} %get-tuple-element.5), channel_id=1, source_target_pairs={{0,1},{1,0},{2,3},{3,2},{4,5},{5,4},{6,7},{7,6},{8,9},{9,8},{10,11... | collective-permute-start | bytes 258056 | tf_op jit(solution)/shard_map/ppermute | solution.py:31
  159.4 2.5 %copy-start.4 = (f32[1,4,176,304]{2,3,1,0:T(8,128)S(1)}, f32[1,4,176,304]{2,3,1,0:T(8,128)}, u32[]{:S(2)}) copy-start(f32[1,4,176,304]{2,3,1,0:T(8,128)} %copy-done.3) | copy-start | bytes 2568196
  159.4 2.6 %copy-start.10 = (f32[1,4,24,304]{2,3,1,0:T(8,128)S(1)}, f32[1,4,24,304]{2,3,1,0:T(8,128)}, u32[]{:S(2)}) copy-start(f32[1,4,24,304]{2,3,1,0:T(8,128)} %copy.118) | copy-start | bytes 350212
  159.4 2.6 %copy-start.11 = (f32[1,4,24,304]{2,3,1,0:T(8,128)S(1)}, f32[1,4,24,304]{2,3,1,0:T(8,128)}, u32[]{:S(2)}) copy-start(f32[1,4,24,304]{2,3,1,0:T(8,128)} %copy.119) | copy-start | bytes 350212
  159.4 4.4 %collective-permute-start.3 = (f32[1,4,224,24]{2,3,1,0:T(8,128)S(1)}, f32[1,4,224,24]{2,3,1,0:T(8,128)S(1)}, u32[]{:S(2)}, u32[]{:S(2)}) collective-permute-start(f32[1,4,224,24]{2,3,1,0:T(8,128)S(1)} %get-tuple-element.6), channel_id=1, source_target_pairs={{1,0},{0,1},{3,2},{2,3},{5,4},{4,5},{7,6},{6,7},{9,8},{8,9},{11,10... | collective-permute-start | bytes 258056 | tf_op jit(solution)/shard_map/ppermute | solution.py:34
  161.9 1.9 copy-start.12
  161.9 1.9 copy-start.13
  163.8 0.9 copy-start.22
  164.6 1.2 copy-start.21
  166.6 9.2 %collective-permute-start.4 = (f32[1,4,32,2,256]{4,1,3,2,0:T(4,128)S(1)}, f32[1,4,32,2,256]{4,1,3,2,0:T(4,128)S(1)}, u32[]{:S(2)}, u32[]{:S(2)}) collective-permute-start(f32[1,4,32,2,256]{4,1,3,2,0:T(4,128)S(1)} %get-tuple-element.24), channel_id=1, source_target_pairs={{0,8},{8,0},{16,24},{24,16},{1,9},{9,1},{17,25},{25,17},{2,10},{10... | collective-permute-start | bytes 786440 | tf_op jit(solution)/shard_map/ppermute | solution.py:22
  168.1 16.2 %collective-permute-start.10 = (f32[1,4,32,2,256]{4,1,2,3,0:T(4,128)S(1)}, f32[1,4,32,2,256]{4,1,2,3,0:T(4,128)S(1)}, u32[]{:S(2)}, u32[]{:S(2)}) collective-permute-start(f32[1,4,32,2,256]{4,1,2,3,0:T(4,128)S(1)} %select_bitcast_fusion.1), channel_id=1, source_target_pairs={{0,8},{8,0},{16,24},{24,16},{1,9},{9,1},{17,25},{25,17},{2,10},{10... | collective-permute-start | bytes 786440 | tf_op jit(solution)/shard_map/ppermute | solution.py:22
  169.4 21.0 %collective-permute-start.16 = (f32[1,4,32,2,256]{4,1,2,3,0:T(4,128)S(1)}, f32[1,4,32,2,256]{4,1,2,3,0:T(4,128)S(1)}, u32[]{:S(2)}, u32[]{:S(2)}) collective-permute-start(f32[1,4,32,2,256]{4,1,2,3,0:T(4,128)S(1)} %select_bitcast_fusion), channel_id=1, source_target_pairs={{0,8},{8,0},{16,24},{24,16},{1,9},{9,1},{17,25},{25,17},{2,10},{10... | collective-permute-start | bytes 786440 | tf_op jit(solution)/shard_map/ppermute | solution.py:22
  176.4 15.7 %collective-permute-start.5 = (f32[1,4,32,1,256]{4,1,2,3,0:T(4,128)S(1)}, f32[1,4,32,1,256]{4,1,2,3,0:T(4,128)S(1)}, u32[]{:S(2)}, u32[]{:S(2)}) collective-permute-start(f32[1,4,32,1,256]{4,1,2,3,0:T(4,128)S(1)} %select_bitcast_fusion.5), channel_id=1, source_target_pairs={{0,16},{16,0},{8,24},{24,8},{1,17},{17,1},{9,25},{25,9},{2,18},{18... | collective-permute-start | bytes 393224 | tf_op jit(solution)/shard_map/ppermute | solution.py:22
  184.8 14.7 %collective-permute-start.11 = (f32[1,4,32,1,256]{4,1,2,3,0:T(4,128)S(1)}, f32[1,4,32,1,256]{4,1,2,3,0:T(4,128)S(1)}, u32[]{:S(2)}, u32[]{:S(2)}) collective-permute-start(f32[1,4,32,1,256]{4,1,2,3,0:T(4,128)S(1)} %select_bitcast_fusion.4), channel_id=1, source_target_pairs={{0,16},{16,0},{8,24},{24,8},{1,17},{17,1},{9,25},{25,9},{2,18},{18... | collective-permute-start | bytes 393224 | tf_op jit(solution)/shard_map/ppermute | solution.py:22
  191.1 10.0 %collective-permute-start.17 = (f32[1,4,32,1,256]{4,1,2,3,0:T(4,128)S(1)}, f32[1,4,32,1,256]{4,1,2,3,0:T(4,128)S(1)}, u32[]{:S(2)}, u32[]{:S(2)}) collective-permute-start(f32[1,4,32,1,256]{4,1,2,3,0:T(4,128)S(1)} %select_bitcast_fusion.3), channel_id=1, source_target_pairs={{0,16},{16,0},{8,24},{24,8},{1,17},{17,1},{9,25},{25,9},{2,18},{18... | collective-permute-start | bytes 393224 | tf_op jit(solution)/shard_map/ppermute | solution.py:22
where the time goes:
time: 205 us; the launch traced here: 203 us
  local copies, waits for them, and re-layouts  75.4 us (37%)
  other arithmetic  45.6 us (22%)
  waiting for transfers between devices  21.7 us (11%)
  starting transfers between devices  21.5 us (10%)
  between operations  20.3 us (10%)
  matrix products  18.2 us (9%)
    dynamic_update_slice x6, local copies, waits for them, and re-layouts, render_view(): lax.dynamic_update_slice(canvas, current + shaded[:, brick_index], corner)  42.4 us
    ppermute x6, waiting for transfers between devices, partner(): return lax.ppermute(block, axis, route)  21.7 us
    dot_general x3, matrix products, render_view(): jnp.einsum('zty,fzybu->fbztu', row_weights, resampled, preferred_element_...  18.2 us
    ppermute x6, starting transfers between devices, partner(): return lax.ppermute(block, axis, route)  9.79 us
    slice x6, local copies, waits for them, and re-layouts, extended(): lax.slice_in_dim(block, block.shape[dim] - width, None, axis=dim)  9.04 us
    mul x3, other arithmetic, integrate(): colors = jnp.sum(footprint[1:] * weight, axis=-3)  7.55 us
    ppermute x6, starting transfers between devices, extended(): lax.ppermute(lax.slice_in_dim(block, 0, width, axis=dim), axis, backward)  7.52 us
    broadcast_in_dim x3, other arithmetic, local(): canvas[None]  6.22 us
  transfers between devices with their start and end apart: 18, of which 5 were waited for; matrix products, arithmetic and copies ran while one was open for 46% of the time, Pallas kernels for 0%

commit v1 on v0

v1 whole, which is shorter than its diff:
```python
import functools
import math
import jax
import jax.numpy as jnp
from jax import lax
from jax.experimental import pallas as pl
from jax.experimental.pallas import tpu as pltpu
from jax.sharding import PartitionSpec as P

MARGIN = 16
JIT = 8
VIEWS = 3

SHEAR_ROWS = (0.75, -0.5, 0.25)
SHEAR_COLS = (-0.25, 0.625, -0.875)

TILE = 8
BF = jnp.bfloat16
F32 = jnp.float32
SMEM = pl.BlockSpec(memory_space=pltpu.SMEM)
VMEM = pl.BlockSpec(memory_space=pltpu.VMEM)
ANY = pl.BlockSpec(memory_space=pl.ANY)


def shared_spill(view, slices, phases):
    reach = abs(SHEAR_ROWS[view]) * (MARGIN - 2) * (slices - 1) / slices + JIT + 1
    need = -(-(math.ceil(reach) - 1) // phases)
    assert need <= TILE and phases & (phases - 1) == 0
    return 2 * need <= TILE


def canvas_rows(view, slices, phases, length):
    return length + (1 if shared_spill(view, slices, phases) else 2) * TILE * phases


def render_kernel(view, phases, offs, order, dens, emis, home, rim, dbuf, ebuf, drow, dcol, hs, rs, sem):
    slices, length, columns = dens.shape
    bricks = columns // length
    half = length // 2
    quota = length // phases
    back = order[view, 0] == 1

    def slice_at(k):
        return jnp.where(back, slices - 1 - k, k)

    def copies(z):
        return (
            pltpu.make_async_copy(dens.at[z], dbuf.at[z], sem.at[0, z]),
            pltpu.make_async_copy(emis.at[:, z], ebuf.at[:, z], sem.at[1, z]),
        )

    for k in range(slices):
        for copy in copies(slice_at(k)):
            copy.start()

    def row_table(count, place):
        shape = (phases, count, length)
        phase = lax.broadcasted_iota(jnp.int32, shape, 0)
        spot = lax.broadcasted_iota(jnp.int32, shape, 1)
        source = lax.broadcasted_iota(jnp.int32, shape, 2)
        return (place(spot) * phases + phase - source).astype(F32).reshape(phases * count, length)

    spill = TILE * phases
    drow[0:length] = row_table(quota, lambda spot: spot)
    if drow.shape[0] == length + spill:
        drow[length:] = row_table(
            TILE, lambda spot: jnp.where(spot < TILE // 2, spot + quota, spot - TILE)
        )
    else:
        drow[length : length + spill] = row_table(TILE, lambda spot: spot - TILE)
        drow[length + spill :] = row_table(TILE, lambda spot: spot + quota)
    lane = lax.broadcasted_iota(jnp.int32, (length, length), 1)
    source = lax.broadcasted_iota(jnp.int32, (length, length), 0)
    dcol[0] = (lane - source).astype(F32)
    dcol[1] = (jnp.where(lane < half, lane + length, lane - length) - source).astype(F32)
    dcol[2] = (jnp.where(lane < half, lane - half, lane + half) - source).astype(F32)
    for ref in (home, rim):
        ref[0:3] = jnp.zeros((3,) + ref.shape[1:], F32)
        ref[3] = jnp.ones(ref.shape[1:], F32)

    def step(k, carry):
        z = slice_at(k)
        for copy in copies(z):
            copy.wait()
        spot = (2 * z - (slices - 1)).astype(F32)
        row_shift = spot * (SHEAR_ROWS[view] * (MARGIN - 2) / slices)
        col_shift = spot * (SHEAR_COLS[view] * (MARGIN - 2) / slices)
        row_weights = []
        for b in range(bricks):
            part = slice(b * length, (b + 1) * length)
            left = offs[view, 1, 0, 0, b].astype(F32) + col_shift
            top = offs[view, 0, 0, 0, b].astype(F32) + row_shift
            distance = jnp.concatenate([dcol[0], dcol[1 + b]], 1) - left
            col_weights = jnp.maximum(0.0, 1.0 - jnp.abs(distance)).astype(BF)
            cells = [dbuf[z, :, part]] + [ebuf[c, z, :, part] for c in range(3)]
            for f in range(4):
                resampled = jnp.dot(cells[f], col_weights, preferred_element_type=F32).astype(BF)
                field = slice(f * length, (f + 1) * length)
                hs[b, :, field] = resampled[:, :length]
                rs[part, field] = resampled[:, length:]
            row_weights.append(jnp.maximum(0.0, 1.0 - jnp.abs(drow[...] - top)).astype(BF))

        def shade(footprint, ref, part):
            through = ref[3, :, part]
            passed = through * jnp.exp(-footprint[:, :length])
            weight = through - passed
            ref[3, :, part] = passed
            for c in range(3):
                color = footprint[:, (c + 1) * length : (c + 2) * length]
                ref[c, :, part] = ref[c, :, part] + color * weight

        for b in range(bricks):
            shade(
                jnp.dot(row_weights[b], hs[b], preferred_element_type=F32),
                home,
                slice(b * length, (b + 1) * length),
            )
        both = jnp.concatenate(row_weights, 1)
        shade(jnp.dot(both, rs[...], preferred_element_type=F32), rim, slice(0, length))
        return carry

    lax.fori_loop(0, slices, step, 0)


def render(view, phases, offsets, orders, density, emission):
    slices, length, columns = density.shape
    rows = canvas_rows(view, slices, phases, length)
    bricks = columns // length
    assert bricks == 2 and length == 128
    return pl.pallas_call(
        functools.partial(render_kernel, view, phases),
        out_shape=(
            jax.ShapeDtypeStruct((4, rows, columns), F32),
            jax.ShapeDtypeStruct((4, rows, length), F32),
        ),
        in_specs=[SMEM, SMEM, ANY, ANY],
        out_specs=(VMEM, VMEM),
        scratch_shapes=[
            pltpu.VMEM(density.shape, BF),
            pltpu.VMEM(emission.shape, BF),
            pltpu.VMEM((rows, length), F32),
            pltpu.VMEM((3, length, length), F32),
            pltpu.VMEM((bricks, length, 4 * length), BF),
            pltpu.VMEM((bricks * length, 4 * length), BF),
            pltpu.SemaphoreType.DMA((2, slices)),
        ],
        name=f"render{view}",
    )(offsets, orders, density, emission)


def joined(channel, one, other):
    return one * other if channel == 3 else one + other


def fold_kernel(shared, phases, home, rim, low, high, *outs):
    rows, columns = home.shape[1:]
    lanes = columns // 2
    half, quarter = lanes // 2, lanes // 4
    quota = (rows - (1 if shared else 2) * TILE * phases) // phases
    length = quota * phases
    inner, (edge, up, down) = outs[:-3], outs[-3:]
    me = lax.axis_index("depth")

    def folded(c, start, count):
        part = pl.ds(start, count)
        lane = lax.broadcasted_iota(jnp.int32, (count, lanes), 1)
        neutral = 1.0 if c == 3 else 0.0
        own = rim[c, part]
        first = jnp.where(lane < half, own, low[c, part])
        first = jnp.where((lane >= quarter) & (lane < lanes - quarter), first, neutral)
        second = jnp.where(lane < half, own, high[c, part])
        second = jnp.where((lane < quarter) | (lane >= lanes - quarter), second, neutral)
        return (
            joined(c, home[c, part, 0:lanes], pltpu.roll(first, half, 1)),
            joined(c, home[c, part, lanes:columns], second),
        )

    for c in range(4):
        for p in range(phases):
            for side, start in enumerate((0, quota - TILE)):
                spot = slice(side * TILE, (side + 1) * TILE)
                one, other = folded(c, p * quota + start, TILE)
                edge[c, p, spot, 0:lanes] = one
                edge[c, p, spot, lanes:columns] = other
        for k, out in enumerate(inner):
            start = pl.multiple_of((me ^ k) * quota + TILE, TILE)
            one, other = folded(c, start, quota - 2 * TILE)
            out[c, :, 0:lanes] = one
            out[c, :, lanes:columns] = other
        if shared:
            sub = lax.broadcasted_iota(jnp.int32, (TILE, lanes), 0)
            for j in range(phases // 2):
                one = folded(c, length + 2 * j * TILE, TILE)
                other = folded(c, length + (2 * j + 1) * TILE, TILE)
                for n in range(2):
                    turned = pltpu.roll(other[n], TILE // 2, 0)
                    part = slice(n * lanes, (n + 1) * lanes)
                    up[c, j, :, part] = jnp.where(sub < TILE // 2, turned, one[n])
                    down[c, j, :, part] = jnp.where(sub < TILE // 2, one[n], turned)
        else:
            for p in range(phases):
                for n, out in enumerate((up, down)):
                    one, other = folded(c, length + (n * phases + p) * TILE, TILE)
                    out[c, p, :, 0:lanes] = one
                    out[c, p, :, lanes:columns] = other


def fold(view, slices, length, phases, home, rim, low, high):
    columns = home.shape[2]
    shared = shared_spill(view, slices, phases)
    quota = length // phases
    packs = phases // 2 if shared else phases
    shapes = [(4, quota - 2 * TILE, columns)] * (phases if quota > 2 * TILE else 0)
    shapes += [(4, phases, 2 * TILE, columns)] + [(4, packs, TILE, columns)] * 2
    outs = pl.pallas_call(
        functools.partial(fold_kernel, shared, phases),
        out_shape=tuple(jax.ShapeDtypeStruct(shape, F32) for shape in shapes),
        in_specs=[VMEM] * 4,
        out_specs=(VMEM,) * len(shapes),
        name=f"fold{view}",
    )(home, rim, low, high)
    return outs[:-3], *outs[-3:]


def edge_kernel(shared, phases, edge, above, below, *outs):
    me = lax.axis_index("depth")
    for k in range(phases):
        p = me ^ k
        for c in range(4):
            if shared:
                neutral = 1.0 if c == 3 else 0.0
                sub = lax.broadcasted_iota(jnp.int32, above.shape[2:], 0)
                odd = (p & 1) == 1
                top, bottom = above[c, p >> 1], below[c, p >> 1]
                top = jnp.where(odd, pltpu.roll(top, TILE // 2, 0), top)
                bottom = jnp.where(odd, pltpu.roll(bottom, TILE // 2, 0), bottom)
                top = jnp.where(sub < TILE // 2, top, neutral)
                bottom = jnp.where(sub < TILE // 2, neutral, bottom)
            else:
                top, bottom = above[c, p], below[c, p]
            outs[k][c, 0:TILE] = joined(c, edge[c, p, 0:TILE], top)
            outs[k][c, TILE:] = joined(c, edge[c, p, TILE:], bottom)


def finish_edges(view, shared, phases, edge, above, below):
    shape = jax.ShapeDtypeStruct((4, 2 * TILE, edge.shape[3]), F32)
    return pl.pallas_call(
        functools.partial(edge_kernel, shared, phases),
        out_shape=(shape,) * phases,
        in_specs=[VMEM] * 3,
        out_specs=(VMEM,) * phases,
        name=f"edge{view}",
    )(edge, above, below)


def over_kernel(view, phases, layers, order, *refs):
    edges, inner = refs[:phases], refs[phases : layers]
    out, stage, sem = refs[-3:]
    backward = order[view, 0] == 1
    me = lax.axis_index("depth")
    count = stage.shape[1]

    def composed(parts):
        bit = 0
        while len(parts) > 1:
            first = jnp.logical_xor((me >> bit & 1) == 0, backward)
            paired = []
            for one, other in zip(parts[0::2], parts[1::2]):
                front = [jnp.where(first, a, b) for a, b in zip(one, other)]
                rear = [jnp.where(first, b, a) for a, b in zip(one, other)]
                paired.append([f + front[3] * r for f, r in zip(front[:3], rear[:3])] + [front[3] * rear[3]])
            parts = paired
            bit += 1
        return parts[0]

    for start, refset, at, size in (
        (0, edges, 0, TILE),
        (TILE, inner, 0, count - 2 * TILE),
        (count - TILE, edges, TILE, TILE),
    ):
        if size == 0:
            continue
        pixels = composed([[ref[c, at : at + size] for c in range(4)] for ref in refset])
        for c in range(4):
            stage[c, start : start + size] = pixels[c]
    copy = pltpu.make_async_copy(stage, out.at[view], sem)
    copy.start()
    copy.wait()


def composite(view, phases, orders, inner, edges, image):
    columns = edges[0].shape[2]
    quota = (inner[0].shape[1] if inner else 0) + 2 * TILE
    operands = [orders, *edges, *inner]
    specs = [SMEM] + [VMEM] * (phases + len(inner))
    aliases = {}
    if image is not None:
        operands.append(image)
        specs.append(ANY)
        aliases = {len(operands) - 1: 0}
    return pl.pallas_call(
        functools.partial(over_kernel, view, phases, phases + len(inner)),
        out_shape=jax.ShapeDtypeStruct((VIEWS, 4, quota, columns), F32),
        in_specs=specs,
        out_specs=ANY,
        scratch_shapes=[pltpu.VMEM((4, quota, columns), F32), pltpu.SemaphoreType.DMA],
        input_output_aliases=aliases,
        name=f"over{view}",
    )(*operands)


def shifted(block, axis, step):
    count = lax.axis_size(axis)
    return lax.ppermute(block, axis, [(i, (i + step) % count) for i in range(count)])


def spread(blocks):
    count = lax.axis_size("depth")
    return [
        block if k == 0 else lax.ppermute(block, "depth", [(i, i ^ k) for i in range(count)])
        for k, block in enumerate(blocks)
    ]


def local(density, emission, offsets, view_order):
    slices, length = density.shape[:2]
    phases = lax.axis_size("depth")
    image = None
    for view in range(VIEWS):
        home, rim = render(view, phases, offsets, view_order, density, emission)
        low = shifted(rim, "col", 1)
        high = low if lax.axis_size("col") == 2 else shifted(rim, "col", -1)
        inner, edge, up, down = fold(view, slices, length, phases, home, rim, low, high)
        inner = spread(inner)
        above = shifted(down, "row", 1)
        below = shifted(up, "row", -1)
        edges = spread(
            finish_edges(view, shared_spill(view, slices, phases), phases, edge, above, below)
        )
        image = composite(view, phases, view_order, inner, edges, image)
    return image[:, :, :, None, :]


def solution(mesh):
    return jax.shard_map(
        local,
        mesh=mesh,
        in_specs=(
            P("depth", "row", "col"),
            P(None, "depth", "row", "col"),
            P(None, None, "depth", "row", "col"),
            P(None, "row"),
        ),
        out_specs=P(None, None, "row", "depth", "col"),
        check_vma=False,
    )
```

time: 205 us -> 87.8 us (0.43)
  local copies, waits for them, and re-layouts: 75.4 us -> 6.29 us
  other arithmetic: 45.6 us -> 0 us
  Pallas kernels: 0 us -> 39.8 us
  waiting for transfers between devices: 21.7 us -> 0.92 us
  between operations: 20.3 us -> 0.3 us
  starting transfers between devices: 21.5 us -> 39.8 us
  matrix products: 18.2 us -> 0 us
    dynamic_update_slice x6 -> x0, local copies, waits for them, and re-layouts: 42.4 us -> none  [render_view(): lax.dynamic_update_slice(canvas, current + shaded[:, brick_index], corner)]
    pallas_call x0 -> x12, Pallas kernels: none -> 39.8 us  [the longest x3 21.9 us: render(): pl.pallas_call(functools.partial(render_kernel, view, phases), out_shape=...]
    ppermute x18 -> x27, waiting for transfers between devices: 21.7 us -> 0.92 us  [the longest x18 0.9 us: spread(): lax.ppermute(block, 'depth', [(i, i ^ k) for i in range(count)])]
    ppermute x18 -> x27, starting transfers between devices: 21.5 us -> 39.8 us  [the longest x18 29.2 us: spread(): lax.ppermute(block, 'depth', [(i, i ^ k) for i in range(count)])]
    dot_general x3 -> x0, matrix products: 18.2 us -> none  [render_view(): jnp.einsum('zty,fzybu->fbztu', row_weights, resampled, preferred_element_...]
    slice x19 -> x0, local copies, waits for them, and re-layouts: 15.4 us -> none  [the longest x6 9.04 us: extended(): lax.slice_in_dim(block, block.shape[dim] - width, None, axis=dim)]
    ppermute x6 -> x0, local copies, waits for them, and re-layouts: 10.1 us -> none  [the longest x3 5.93 us: extended(): lax.ppermute(lax.slice_in_dim(block, 0, width, axis=dim), axis, backward)]
    reduce_sum x6 -> x0, other arithmetic: 9.35 us -> none  [the longest x3 5.89 us: integrate(): total_depth = jnp.sum(extinction, axis=-3)]
  transfers between devices with their start and end apart: 18 -> 27, of which waited for: 5 -> 2; matrix products, arithmetic and copies ran while one was open for 46% -> 0% of each run, Pallas kernels for 0% -> 35%
where the time goes in v1:
time: 87.8 us; the launch traced here: 87.1 us
  Pallas kernels  39.8 us (45%)
  starting transfers between devices  39.8 us (45%)
  local copies, waits for them, and re-layouts  6.29 us (7%)
  waiting for transfers between devices  0.92 us (1%)
    ppermute x18, starting transfers between devices, spread(): lax.ppermute(block, 'depth', [(i, i ^ k) for i in range(count)])  29.2 us
    pallas_call x3, Pallas kernels, render(): pl.pallas_call(functools.partial(render_kernel, view, phases), out_shape=...  21.9 us
    ppermute x9, starting transfers between devices, shifted(): lax.ppermute(block, axis, [(i, (i + step) % count) for i in range(count)])  10.6 us
    pallas_call x3, Pallas kernels, fold(): pl.pallas_call(functools.partial(fold_kernel, shared, phases), out_shape=...  7.28 us
    pallas_call x3, Pallas kernels, composite(): pl.pallas_call(functools.partial(over_kernel, view, phases, phases + len(...  5.41 us
    pallas_call x3, Pallas kernels, finish_edges(): pl.pallas_call(functools.partial(edge_kernel, shared, phases), out_shape=...  5.22 us
    unnamed x64, local copies, waits for them, and re-layouts  4.15 us
    broadcast_in_dim x1, local copies, waits for them, and re-layouts, local(): return image[:, :, :, None, :]  2.15 us
  transfers between devices with their start and end apart: 27, of which 2 were waited for; matrix products, arithmetic and copies ran while one was open for 0% of the time, Pallas kernels for 35%

profile of v1, /device:TPU:0, one launch (start us, length us, event | category | flops | bytes accessed | tf_op | source)
XLA Modules:
  0.0 87.1 jit_solution(3668911895742386821)
XLA Ops:
  0.0 1.3 %copy.15.order = s32[3,1]{1,0:T(4,128)} copy(s32[3,1]{0,1:T(1,128)} %param.7) | data formatting | bytes 24 | tf_op args[3]
  1.3 1.4 %copy.7.offs = s32[3,2,1,1,2]{4,3,2,1,0:T(1,128)} copy(s32[3,2,1,1,2]{0,4,3,2,1:T(2,128)} %param.6) | data formatting | bytes 96 | tf_op args[2]
  2.7 7.4 %render0.1 = (f32[4,192,256]{2,1,0:T(8,128)}, f32[4,192,128]{2,1,0:T(8,128)}) custom-call(s32[3,2,1,1,2]{4,3,2,1,0:T(1,128)} %copy.7.offs, s32[3,1]{1,0:T(4,128)} %copy.15.order, bf16[8,128,256]{2,1,0:T(8,128)(2,1)} %dens.5, bf16[3,8,128,256]{3,2,1,0:T(8,128)(2,1)} %emis.5), custom_call_target="tpu_custom_call" | custom-call | tf_op jit(solution)/shard_map/render0/pallas_call | solution.py:130
  10.1 0.6 collective-permute-start.18
  10.7 7.2 %render1.1 = (f32[4,160,256]{2,1,0:T(8,128)}, f32[4,160,128]{2,1,0:T(8,128)}) custom-call(s32[3,2,1,1,2]{4,3,2,1,0:T(1,128)} %copy.7.offs, s32[3,1]{1,0:T(4,128)} %copy.15.order, bf16[8,128,256]{2,1,0:T(8,128)(2,1)} %dens.5, bf16[3,8,128,256]{3,2,1,0:T(8,128)(2,1)} %emis.5), custom_call_target="tpu_custom_call" | custom-call | tf_op jit(solution)/shard_map/render1/pallas_call | solution.py:130
  17.9 0.1 collective-permute-start.9
  18.0 7.2 %render2.1 = (f32[4,160,256]{2,1,0:T(8,128)}, f32[4,160,128]{2,1,0:T(8,128)}) custom-call(s32[3,2,1,1,2]{4,3,2,1,0:T(1,128)} %copy.7.offs, s32[3,1]{1,0:T(4,128)} %copy.15.order, bf16[8,128,256]{2,1,0:T(8,128)(2,1)} %dens.5, bf16[3,8,128,256]{3,2,1,0:T(8,128)(2,1)} %emis.5), custom_call_target="tpu_custom_call" | custom-call | tf_op jit(solution)/shard_map/render2/pallas_call | solution.py:130
  25.2 0.6 collective-permute-start
  25.8 0.7 copy-done.2
  26.5 2.3 %fold1.1 = (f32[4,16,256]{2,1,0:T(8,128)}, f32[4,16,256]{2,1,0:T(8,128)}, f32[4,16,256]{2,1,0:T(8,128)}, f32[4,16,256]{2,1,0:T(8,128)}, f32[4,4,16,256]{3,2,1,0:...) custom-call(f32[4,160,256]{2,1,0:T(8,128)} %get-tuple-element.57.home, ...), custom_call_target="tpu_custom_call" | custom-call | tf_op jit(solution)/shard_map/fold1/pallas_call | solution.py:215
  28.9 2.5 %collective-permute-start.10 = (f32[4,2,8,256]{3,2,1,0:T(8,128)}, f32[4,2,8,256]{3,2,1,0:T(8,128)S(1)}, u32[]{:S(2)}, u32[]{:S(2)}) collective-permute-start(f32[4,2,8,256]{3,2,1,0:T(8,128)} %get-tuple-element.60), channel_id=1, source_target_pairs={{0,2},{2,4},{4,6},{6,0},{1,3},{3,5},{5,7},{7,1},{8,10},{10,12},{12... | collective-permute-start | bytes 196616 | tf_op jit(solution)/shard_map/ppermute | solution.py:314
  31.4 1.0 %collective-permute-start.11 = (f32[4,2,8,256]{3,2,1,0:T(8,128)}, f32[4,2,8,256]{3,2,1,0:T(8,128)S(1)}, u32[]{:S(2)}, u32[]{:S(2)}) collective-permute-start(f32[4,2,8,256]{3,2,1,0:T(8,128)} %get-tuple-element.61), channel_id=1, source_target_pairs={{0,6},{2,0},{4,2},{6,4},{1,7},{3,1},{5,3},{7,5},{8,14},{10,8},{12,... | collective-permute-start | bytes 196616 | tf_op jit(solution)/shard_map/ppermute | solution.py:314
  32.4 2.0 %collective-permute-start.15 = (f32[4,16,256]{2,1,0:T(8,128)}, f32[4,16,256]{2,1,0:T(8,128)S(1)}, u32[]{:S(2)}, u32[]{:S(2)}) collective-permute-start(f32[4,16,256]{2,1,0:T(8,128)} %get-tuple-element.67), channel_id=1, source_target_pairs={{0,8},{8,0},{16,24},{24,16},{1,9},{9,1},{17,25},{25,17},{2,10},{10... | collective-permute-start | bytes 196616 | tf_op jit(solution)/shard_map/ppermute | solution.py:320
  34.4 2.6 %collective-permute-start.16 = (f32[4,16,256]{2,1,0:T(8,128)}, f32[4,16,256]{2,1,0:T(8,128)S(1)}, u32[]{:S(2)}, u32[]{:S(2)}) collective-permute-start(f32[4,16,256]{2,1,0:T(8,128)} %get-tuple-element.68), channel_id=1, source_target_pairs={{0,16},{8,24},{16,0},{24,8},{1,17},{9,25},{17,1},{25,9},{2,18},{10... | collective-permute-start | bytes 196616 | tf_op jit(solution)/shard_map/ppermute | solution.py:320
  37.0 2.6 %fold0.1 = (f32[4,16,256]{2,1,0:T(8,128)}, f32[4,16,256]{2,1,0:T(8,128)}, f32[4,16,256]{2,1,0:T(8,128)}, f32[4,16,256]{2,1,0:T(8,128)}, f32[4,4,16,256]{3,2,1,0:...) custom-call(f32[4,192,256]{2,1,0:T(8,128)} %get-tuple-element.70.home, ...), custom_call_target="tpu_custom_call" | custom-call | tf_op jit(solution)/shard_map/fold0/pallas_call | solution.py:215
  39.6 0.6 collective-permute-start.19
  40.2 2.4 %collective-permute-start.20 = (f32[4,4,8,256]{3,2,1,0:T(8,128)}, f32[4,4,8,256]{3,2,1,0:T(8,128)S(1)}, u32[]{:S(2)}, u32[]{:S(2)}) collective-permute-start(f32[4,4,8,256]{3,2,1,0:T(8,128)} %get-tuple-element.74), channel_id=1, source_target_pairs={{0,6},{2,0},{4,2},{6,4},{1,7},{3,1},{5,3},{7,5},{8,14},{10,8},{12,... | collective-permute-start | bytes 393224 | tf_op jit(solution)/shard_map/ppermute | solution.py:314
  42.6 2.4 %fold2.1 = (f32[4,16,256]{2,1,0:T(8,128)}, f32[4,16,256]{2,1,0:T(8,128)}, f32[4,16,256]{2,1,0:T(8,128)}, f32[4,16,256]{2,1,0:T(8,128)}, f32[4,4,16,256]{3,2,1,0:...) custom-call(f32[4,160,256]{2,1,0:T(8,128)} %get-tuple-element.44.home, ...), custom_call_target="tpu_custom_call" | custom-call | tf_op jit(solution)/shard_map/fold2/pallas_call | solution.py:215
  45.0 0.7 collective-permute-start.17
  45.7 0.1 collective-permute-start.1
  45.8 2.8 %collective-permute-start.2 = (f32[4,2,8,256]{3,2,1,0:T(8,128)}, f32[4,2,8,256]{3,2,1,0:T(8,128)S(1)}, u32[]{:S(2)}, u32[]{:S(2)}) collective-permute-start(f32[4,2,8,256]{3,2,1,0:T(8,128)} %get-tuple-element.48), channel_id=1, source_target_pairs={{0,6},{2,0},{4,2},{6,4},{1,7},{3,1},{5,3},{7,5},{8,14},{10,8},{12,... | collective-permute-start | bytes 196616 | tf_op jit(solution)/shard_map/ppermute | solution.py:314
  48.6 1.7 %edge1.1 = (f32[4,16,256]{2,1,0:T(8,128)}, f32[4,16,256]{2,1,0:T(8,128)}, f32[4,16,256]{2,1,0:T(8,128)}, f32[4,16,256]{2,1,0:T(8,128)}) custom-call(f32[4,4,16,256]{3,2,1,0:T(8,128)} %get-tuple-element.59.edge, f32[4,2,8,256]{3,2,1,0:T(8,128)} %copy-done.25, f32[4,2,8,256]{3,2,1,0:T(8,128)} %copy-done.26), custom_call_target="tpu_custom_call" | custom-call | tf_op jit(solution)/shard_map/edge1/pallas_call | solution.py:247
  50.3 0.8 collective-permute-done.17.refs_7_
  51.2 2.1 %collective-permute-start.24 = (f32[4,16,256]{2,1,0:T(8,128)S(1)}, f32[4,16,256]{2,1,0:T(8,128)S(1)}, u32[]{:S(2)}, u32[]{:S(2)}) collective-permute-start(f32[4,16,256]{2,1,0:T(8,128)S(1)} %copy-done.29), channel_id=1, source_target_pairs={{0,8},{8,0},{16,24},{24,16},{1,9},{9,1},{17,25},{25,17},{2,10},{10... | collective-permute-start | bytes 196616 | tf_op jit(solution)/shard_map/ppermute | solution.py:320
  53.2 1.7 %collective-permute-start.25 = (f32[4,16,256]{2,1,0:T(8,128)S(1)}, f32[4,16,256]{2,1,0:T(8,128)S(1)}, u32[]{:S(2)}, u32[]{:S(2)}) collective-permute-start(f32[4,16,256]{2,1,0:T(8,128)S(1)} %copy-done.28), channel_id=1, source_target_pairs={{0,16},{8,24},{16,0},{24,8},{1,17},{9,25},{17,1},{25,9},{2,18},{10... | collective-permute-start | bytes 196616 | tf_op jit(solution)/shard_map/ppermute | solution.py:320
  54.9 1.0 %collective-permute-start.26 = (f32[4,16,256]{2,1,0:T(8,128)S(1)}, f32[4,16,256]{2,1,0:T(8,128)S(1)}, u32[]{:S(2)}, u32[]{:S(2)}) collective-permute-start(f32[4,16,256]{2,1,0:T(8,128)S(1)} %copy-done.27), channel_id=1, source_target_pairs={{0,24},{8,16},{16,8},{24,0},{1,25},{9,17},{17,9},{25,1},{2,26},{10... | collective-permute-start | bytes 196616 | tf_op jit(solution)/shard_map/ppermute | solution.py:320
  55.9 1.0 %collective-permute-start.12 = (f32[4,16,256]{2,1,0:T(8,128)}, f32[4,16,256]{2,1,0:T(8,128)S(1)}, u32[]{:S(2)}, u32[]{:S(2)}) collective-permute-start(f32[4,16,256]{2,1,0:T(8,128)} %get-tuple-element.63), channel_id=1, source_target_pairs={{0,8},{8,0},{16,24},{24,16},{1,9},{9,1},{17,25},{25,17},{2,10},{10... | collective-permute-start | bytes 196616 | tf_op jit(solution)/shard_map/ppermute | solution.py:320
  56.9 1.8 %edge0.1 = (f32[4,16,256]{2,1,0:T(8,128)}, f32[4,16,256]{2,1,0:T(8,128)}, f32[4,16,256]{2,1,0:T(8,128)}, f32[4,16,256]{2,1,0:T(8,128)}) custom-call(f32[4,4,16,256]{3,2,1,0:T(8,128)} %get-tuple-element.72.edge, f32[4,4,8,256]{3,2,1,0:T(8,128)} %copy-done.3, f32[4,4,8,256]{3,2,1,0:T(8,128)} %copy-done.4), custom_call_target="tpu_custom_call" | custom-call | tf_op jit(solution)/shard_map/edge0/pallas_call | solution.py:247
  58.7 2.6 %collective-permute-start.13 = (f32[4,16,256]{2,1,0:T(8,128)}, f32[4,16,256]{2,1,0:T(8,128)S(1)}, u32[]{:S(2)}, u32[]{:S(2)}) collective-permute-start(f32[4,16,256]{2,1,0:T(8,128)} %get-tuple-element.64), channel_id=1, source_target_pairs={{0,16},{8,24},{16,0},{24,8},{1,17},{9,25},{17,1},{25,9},{2,18},{10... | collective-permute-start | bytes 196616 | tf_op jit(solution)/shard_map/ppermute | solution.py:320
  61.2 0.9 %collective-permute-start.14 = (f32[4,16,256]{2,1,0:T(8,128)}, f32[4,16,256]{2,1,0:T(8,128)S(1)}, u32[]{:S(2)}, u32[]{:S(2)}) collective-permute-start(f32[4,16,256]{2,1,0:T(8,128)} %get-tuple-element.65), channel_id=1, source_target_pairs={{0,24},{8,16},{16,8},{24,0},{1,25},{9,17},{17,9},{25,1},{2,26},{10... | collective-permute-start | bytes 196616 | tf_op jit(solution)/shard_map/ppermute | solution.py:320
  62.2 0.1 collective-permute-start.21
  62.2 3.4 %collective-permute-start.22 = (f32[4,16,256]{2,1,0:T(8,128)}, f32[4,16,256]{2,1,0:T(8,128)S(1)}, u32[]{:S(2)}, u32[]{:S(2)}) collective-permute-start(f32[4,16,256]{2,1,0:T(8,128)} %get-tuple-element.77), channel_id=1, source_target_pairs={{0,16},{8,24},{16,0},{24,8},{1,17},{9,25},{17,1},{25,9},{2,18},{10... | collective-permute-start | bytes 196616 | tf_op jit(solution)/shard_map/ppermute | solution.py:320
  65.6 0.9 %collective-permute-start.23 = (f32[4,16,256]{2,1,0:T(8,128)}, f32[4,16,256]{2,1,0:T(8,128)S(1)}, u32[]{:S(2)}, u32[]{:S(2)}) collective-permute-start(f32[4,16,256]{2,1,0:T(8,128)} %get-tuple-element.78), channel_id=1, source_target_pairs={{0,24},{8,16},{16,8},{24,0},{1,25},{9,17},{17,9},{25,1},{2,26},{10... | collective-permute-start | bytes 196616 | tf_op jit(solution)/shard_map/ppermute | solution.py:320
  66.6 1.7 %edge2.1 = (f32[4,16,256]{2,1,0:T(8,128)}, f32[4,16,256]{2,1,0:T(8,128)}, f32[4,16,256]{2,1,0:T(8,128)}, f32[4,16,256]{2,1,0:T(8,128)}) custom-call(f32[4,4,16,256]{3,2,1,0:T(8,128)} %get-tuple-element.46.edge, f32[4,2,8,256]{3,2,1,0:T(8,128)} %copy-done.23, f32[4,2,8,256]{3,2,1,0:T(8,128)} %copy-done.24), custom_call_target="tpu_custom_call" | custom-call | tf_op jit(solution)/shard_map/edge2/pallas_call | solution.py:247
  68.3 0.7 collective-permute-start.7
  69.0 2.4 %collective-permute-start.8 = (f32[4,16,256]{2,1,0:T(8,128)}, f32[4,16,256]{2,1,0:T(8,128)S(1)}, u32[]{:S(2)}, u32[]{:S(2)}) collective-permute-start(f32[4,16,256]{2,1,0:T(8,128)} %get-tuple-element.56), channel_id=1, source_target_pairs={{0,24},{8,16},{16,8},{24,0},{1,25},{9,17},{17,9},{25,1},{2,26},{10... | collective-permute-start | bytes 196616 | tf_op jit(solution)/shard_map/ppermute | solution.py:320
  71.3 4.8 %collective-permute-start.3 = (f32[4,16,256]{2,1,0:T(8,128)}, f32[4,16,256]{2,1,0:T(8,128)S(1)}, u32[]{:S(2)}, u32[]{:S(2)}) collective-permute-start(f32[4,16,256]{2,1,0:T(8,128)} %get-tuple-element.50), channel_id=1, source_target_pairs={{0,8},{8,0},{16,24},{24,16},{1,9},{9,1},{17,25},{25,17},{2,10},{10... | collective-permute-start | bytes 196616 | tf_op jit(solution)/shard_map/ppermute | solution.py:320
  76.2 2.5 %collective-permute-start.5 = (f32[4,16,256]{2,1,0:T(8,128)}, f32[4,16,256]{2,1,0:T(8,128)S(1)}, u32[]{:S(2)}, u32[]{:S(2)}) collective-permute-start(f32[4,16,256]{2,1,0:T(8,128)} %get-tuple-element.52), channel_id=1, source_target_pairs={{0,24},{8,16},{16,8},{24,0},{1,25},{9,17},{17,9},{25,1},{2,26},{10... | collective-permute-start | bytes 196616 | tf_op jit(solution)/shard_map/ppermute | solution.py:320
  78.7 1.8 %over0.1.refs_8_ = f32[3,4,32,256]{3,2,1,0:T(8,128)} custom-call(s32[3,1]{1,0:T(4,128)} %copy.15.order, f32[4,16,256]{2,1,0:T(8,128)} %get-tuple-element.75.refs_0_, f32[4,16,256]{2,1,0:T(8,128)} %copy-done.8, f32[4,16,256]{2,1,0:T(8,128)} %copy-done.9, f32[4,16,256]{2,1,0:T(8,128)} %copy-done.10, f32[4,16,256]{2,1,0:T(8,128)} %get-tuple-element.79.refs_4_, ...), custom_call_target="tpu_custom_call" | custom-call | tf_op jit(solution)/shard_map/over0/pallas_call | solution.py:301
  80.6 1.8 %over1.1.refs_8_ = f32[3,4,32,256]{3,2,1,0:T(8,128)} custom-call(s32[3,1]{1,0:T(4,128)} %copy.15.order, f32[4,16,256]{2,1,0:T(8,128)} %get-tuple-element.62.refs_0_, f32[4,16,256]{2,1,0:T(8,128)} %copy-done.15, f32[4,16,256]{2,1,0:T(8,128)} %copy-done.16, f32[4,16,256]{2,1,0:T(8,128)} %copy-done.17, ...), custom_call_target="tpu_custom_call", output_to_operand_aliasing={{}: (9, {})} | custom-call | tf_op jit(solution)/shard_map/over1/pallas_call | solution.py:301
  82.5 0.1 collective-permute-done.5.refs_3_
  82.5 0.5 copy-done.18
  83.0 0.0 copy-done.19
  83.0 0.0 copy-done.20
  83.1 0.0 copy-done.21
  83.1 0.1 copy-done.22
  83.2 1.8 %over2.1 = f32[3,4,32,256]{3,2,1,0:T(8,128)} custom-call(s32[3,1]{1,0:T(4,128)} %copy.15.order, f32[4,16,256]{2,1,0:T(8,128)} %get-tuple-element.49.refs_0_, f32[4,16,256]{2,1,0:T(8,128)} %copy-done.20, f32[4,16,256]{2,1,0:T(8,128)} %copy-done.21, f32[4,16,256]{2,1,0:T(8,128)} %copy-done.22, ...), custom_call_target="tpu_custom_call", output_to_operand_aliasing={{}: (9, {})} | custom-call | tf_op jit(solution)/shard_map/over2/pallas_call | solution.py:301
  85.0 2.1 %copy.16 = f32[3,4,32,1,256]{4,3,2,1,0:T(1,128)} copy(f32[3,4,32,1,256]{4,2,1,0,3:T(8,128)} %bitcast.1) | data formatting | bytes 786432 | tf_op jit(solution)/shard_map/broadcast_in_dim | solution.py:341
  (83 shorter events, 0.2 us)
Async XLA Ops:
  10.1 24.3 %collective-permute-start.18 = (f32[4,192,128]{2,1,0:T(8,128)}, f32[4,192,128]{2,1,0:T(8,128)S(1)}, u32[]{:S(2)}, u32[]{:S(2)}) collective-permute-start(f32[4,192,128]{2,1,0:T(8,128)} %get-tuple-element.71.rim), channel_id=1, source_target_pairs={{0,1},{1,0},{2,3},{3,2},{4,5},{5,4},{6,7},{7,6},{8,9},{9,8},{10,11... | collective-permute-start | bytes 1179656 | tf_op jit(solution)/shard_map/ppermute | solution.py:314
  17.9 7.9 %collective-permute-start.9 = (f32[4,160,128]{2,1,0:T(8,128)}, f32[4,160,128]{2,1,0:T(8,128)S(1)}, u32[]{:S(2)}, u32[]{:S(2)}) collective-permute-start(f32[4,160,128]{2,1,0:T(8,128)} %get-tuple-element.58.rim), channel_id=1, source_target_pairs={{0,1},{1,0},{2,3},{3,2},{4,5},{5,4},{6,7},{7,6},{8,9},{9,8},{10,11... | collective-permute-start | bytes 983048 | tf_op jit(solution)/shard_map/ppermute | solution.py:314
  25.2 14.4 %collective-permute-start = (f32[4,160,128]{2,1,0:T(8,128)}, f32[4,160,128]{2,1,0:T(8,128)S(1)}, u32[]{:S(2)}, u32[]{:S(2)}) collective-permute-start(f32[4,160,128]{2,1,0:T(8,128)} %get-tuple-element.45.rim), channel_id=1, source_target_pairs={{0,1},{1,0},{2,3},{3,2},{4,5},{5,4},{6,7},{7,6},{8,9},{9,8},{10,11... | collective-permute-start | bytes 983048 | tf_op jit(solution)/shard_map/ppermute | solution.py:314
  28.9 11.3 %collective-permute-start.10 = (f32[4,2,8,256]{3,2,1,0:T(8,128)}, f32[4,2,8,256]{3,2,1,0:T(8,128)S(1)}, u32[]{:S(2)}, u32[]{:S(2)}) collective-permute-start(f32[4,2,8,256]{3,2,1,0:T(8,128)} %get-tuple-element.60), channel_id=1, source_target_pairs={{0,2},{2,4},{4,6},{6,0},{1,3},{3,5},{5,7},{7,1},{8,10},{10,12},{12... | collective-permute-start | bytes 196616 | tf_op jit(solution)/shard_map/ppermute | solution.py:314
  31.4 13.6 %collective-permute-start.11 = (f32[4,2,8,256]{3,2,1,0:T(8,128)}, f32[4,2,8,256]{3,2,1,0:T(8,128)S(1)}, u32[]{:S(2)}, u32[]{:S(2)}) collective-permute-start(f32[4,2,8,256]{3,2,1,0:T(8,128)} %get-tuple-element.61), channel_id=1, source_target_pairs={{0,6},{2,0},{4,2},{6,4},{1,7},{3,1},{5,3},{7,5},{8,14},{10,8},{12,... | collective-permute-start | bytes 196616 | tf_op jit(solution)/shard_map/ppermute | solution.py:314
  32.4 13.3 %collective-permute-start.15 = (f32[4,16,256]{2,1,0:T(8,128)}, f32[4,16,256]{2,1,0:T(8,128)S(1)}, u32[]{:S(2)}, u32[]{:S(2)}) collective-permute-start(f32[4,16,256]{2,1,0:T(8,128)} %get-tuple-element.67), channel_id=1, source_target_pairs={{0,8},{8,0},{16,24},{24,16},{1,9},{9,1},{17,25},{25,17},{2,10},{10... | collective-permute-start | bytes 196616 | tf_op jit(solution)/shard_map/ppermute | solution.py:320
  34.4 2.6 %copy-start = (f32[4,192,128]{2,1,0:T(8,128)}, f32[4,192,128]{2,1,0:T(8,128)S(1)}, u32[]{:S(2)}) copy-start(f32[4,192,128]{2,1,0:T(8,128)S(1)} %collective-permute-done.18.low.high) | copy-start | bytes 1179652
  34.4 11.4 %collective-permute-start.16 = (f32[4,16,256]{2,1,0:T(8,128)}, f32[4,16,256]{2,1,0:T(8,128)S(1)}, u32[]{:S(2)}, u32[]{:S(2)}) collective-permute-start(f32[4,16,256]{2,1,0:T(8,128)} %get-tuple-element.68), channel_id=1, source_target_pairs={{0,16},{8,24},{16,0},{24,8},{1,17},{9,25},{17,1},{25,9},{2,18},{10... | collective-permute-start | bytes 196616 | tf_op jit(solution)/shard_map/ppermute | solution.py:320
  37.0 8.0 %copy-start.30 = (f32[4,16,256]{2,1,0:T(8,128)S(1)}, f32[4,16,256]{2,1,0:T(8,128)}, u32[]{:S(2)}) copy-start(f32[4,16,256]{2,1,0:T(8,128)} %get-tuple-element.69) | copy-start | bytes 196612
  39.6 11.6 %copy-start.29 = (f32[4,16,256]{2,1,0:T(8,128)S(1)}, f32[4,16,256]{2,1,0:T(8,128)}, u32[]{:S(2)}) copy-start(f32[4,16,256]{2,1,0:T(8,128)} %get-tuple-element.80) | copy-start | bytes 196612
  39.6 13.7 %copy-start.28 = (f32[4,16,256]{2,1,0:T(8,128)S(1)}, f32[4,16,256]{2,1,0:T(8,128)}, u32[]{:S(2)}) copy-start(f32[4,16,256]{2,1,0:T(8,128)} %get-tuple-element.81) | copy-start | bytes 196612
  39.6 15.3 %copy-start.27 = (f32[4,16,256]{2,1,0:T(8,128)S(1)}, f32[4,16,256]{2,1,0:T(8,128)}, u32[]{:S(2)}) copy-start(f32[4,16,256]{2,1,0:T(8,128)} %get-tuple-element.82) | copy-start | bytes 196612
  39.6 3.0 %copy-start.1 = (f32[4,160,128]{2,1,0:T(8,128)}, f32[4,160,128]{2,1,0:T(8,128)S(1)}, u32[]{:S(2)}) copy-start(f32[4,160,128]{2,1,0:T(8,128)S(1)} %collective-permute-done.low.high) | copy-start | bytes 983044
  39.6 15.3 %collective-permute-start.19 = (f32[4,4,8,256]{3,2,1,0:T(8,128)}, f32[4,4,8,256]{3,2,1,0:T(8,128)S(1)}, u32[]{:S(2)}, u32[]{:S(2)}) collective-permute-start(f32[4,4,8,256]{3,2,1,0:T(8,128)} %get-tuple-element.73), channel_id=1, source_target_pairs={{0,2},{2,4},{4,6},{6,0},{1,3},{3,5},{5,7},{7,1},{8,10},{10,12},{12... | collective-permute-start | bytes 393224 | tf_op jit(solution)/shard_map/ppermute | solution.py:314
  40.2 8.4 %copy-start.25 = (f32[4,2,8,256]{3,2,1,0:T(8,128)}, f32[4,2,8,256]{3,2,1,0:T(8,128)S(1)}, u32[]{:S(2)}) copy-start(f32[4,2,8,256]{3,2,1,0:T(8,128)S(1)} %collective-permute-done.10.above) | copy-start | bytes 196612
  40.2 15.7 %collective-permute-start.20 = (f32[4,4,8,256]{3,2,1,0:T(8,128)}, f32[4,4,8,256]{3,2,1,0:T(8,128)S(1)}, u32[]{:S(2)}, u32[]{:S(2)}) collective-permute-start(f32[4,4,8,256]{3,2,1,0:T(8,128)} %get-tuple-element.74), channel_id=1, source_target_pairs={{0,6},{2,0},{4,2},{6,4},{1,7},{3,1},{5,3},{7,5},{8,14},{10,8},{12,... | collective-permute-start | bytes 393224 | tf_op jit(solution)/shard_map/ppermute | solution.py:314
  45.0 3.6 %copy-start.26 = (f32[4,2,8,256]{3,2,1,0:T(8,128)}, f32[4,2,8,256]{3,2,1,0:T(8,128)S(1)}, u32[]{:S(2)}) copy-start(f32[4,2,8,256]{3,2,1,0:T(8,128)S(1)} %collective-permute-done.11.below) | copy-start | bytes 196612
  45.0 6.1 %collective-permute-start.17 = (f32[4,16,256]{2,1,0:T(8,128)S(1)}, f32[4,16,256]{2,1,0:T(8,128)S(1)}, u32[]{:S(2)}, u32[]{:S(2)}) collective-permute-start(f32[4,16,256]{2,1,0:T(8,128)S(1)} %copy-done.30), channel_id=1, source_target_pairs={{0,24},{8,16},{16,8},{24,0},{1,25},{9,17},{17,9},{25,1},{2,26},{10... | collective-permute-start | bytes 196616 | tf_op jit(solution)/shard_map/ppermute | solution.py:320
  45.7 34.8 %copy-start.11 = (f32[4,16,256]{2,1,0:T(8,128)}, f32[4,16,256]{2,1,0:T(8,128)S(1)}, u32[]{:S(2)}) copy-start(f32[4,16,256]{2,1,0:T(8,128)S(1)} %collective-permute-done.15.refs_5_) | copy-start | bytes 196612
  45.7 5.5 %collective-permute-start.1 = (f32[4,2,8,256]{3,2,1,0:T(8,128)}, f32[4,2,8,256]{3,2,1,0:T(8,128)S(1)}, u32[]{:S(2)}, u32[]{:S(2)}) collective-permute-start(f32[4,2,8,256]{3,2,1,0:T(8,128)} %get-tuple-element.47), channel_id=1, source_target_pairs={{0,2},{2,4},{4,6},{6,0},{1,3},{3,5},{5,7},{7,1},{8,10},{10,12},{12... | collective-permute-start | bytes 196616 | tf_op jit(solution)/shard_map/ppermute | solution.py:314
  45.8 34.8 %copy-start.12 = (f32[4,16,256]{2,1,0:T(8,128)}, f32[4,16,256]{2,1,0:T(8,128)S(1)}, u32[]{:S(2)}) copy-start(f32[4,16,256]{2,1,0:T(8,128)S(1)} %collective-permute-done.16.refs_6_) | copy-start | bytes 196612
  45.8 7.5 %collective-permute-start.2 = (f32[4,2,8,256]{3,2,1,0:T(8,128)}, f32[4,2,8,256]{3,2,1,0:T(8,128)S(1)}, u32[]{:S(2)}, u32[]{:S(2)}) collective-permute-start(f32[4,2,8,256]{3,2,1,0:T(8,128)} %get-tuple-element.48), channel_id=1, source_target_pairs={{0,6},{2,0},{4,2},{6,4},{1,7},{3,1},{5,3},{7,5},{8,14},{10,8},{12,... | collective-permute-start | bytes 196616 | tf_op jit(solution)/shard_map/ppermute | solution.py:314
  51.1 29.4 %copy-start.13 = (f32[4,16,256]{2,1,0:T(8,128)}, f32[4,16,256]{2,1,0:T(8,128)S(1)}, u32[]{:S(2)}) copy-start(f32[4,16,256]{2,1,0:T(8,128)S(1)} %collective-permute-done.17.refs_7_) | copy-start | bytes 196612
  51.1 7.5 %collective-permute-start.6 = (f32[4,16,256]{2,1,0:T(8,128)}, f32[4,16,256]{2,1,0:T(8,128)S(1)}, u32[]{:S(2)}, u32[]{:S(2)}) collective-permute-start(f32[4,16,256]{2,1,0:T(8,128)} %get-tuple-element.54), channel_id=1, source_target_pairs={{0,8},{8,0},{16,24},{24,16},{1,9},{9,1},{17,25},{25,17},{2,10},{10... | collective-permute-start | bytes 196616 | tf_op jit(solution)/shard_map/ppermute | solution.py:320
  51.1 15.4 %copy-start.23 = (f32[4,2,8,256]{3,2,1,0:T(8,128)}, f32[4,2,8,256]{3,2,1,0:T(8,128)S(1)}, u32[]{:S(2)}) copy-start(f32[4,2,8,256]{3,2,1,0:T(8,128)S(1)} %collective-permute-done.1.above) | copy-start | bytes 196612
  51.2 10.1 %collective-permute-start.24 = (f32[4,16,256]{2,1,0:T(8,128)S(1)}, f32[4,16,256]{2,1,0:T(8,128)S(1)}, u32[]{:S(2)}, u32[]{:S(2)}) collective-permute-start(f32[4,16,256]{2,1,0:T(8,128)S(1)} %copy-done.29), channel_id=1, source_target_pairs={{0,8},{8,0},{16,24},{24,16},{1,9},{9,1},{17,25},{25,17},{2,10},{10... | collective-permute-start | bytes 196616 | tf_op jit(solution)/shard_map/ppermute | solution.py:320
  53.2 13.3 %copy-start.24 = (f32[4,2,8,256]{3,2,1,0:T(8,128)}, f32[4,2,8,256]{3,2,1,0:T(8,128)S(1)}, u32[]{:S(2)}) copy-start(f32[4,2,8,256]{3,2,1,0:T(8,128)S(1)} %collective-permute-done.2.below) | copy-start | bytes 196612
  53.2 8.9 %collective-permute-start.25 = (f32[4,16,256]{2,1,0:T(8,128)S(1)}, f32[4,16,256]{2,1,0:T(8,128)S(1)}, u32[]{:S(2)}, u32[]{:S(2)}) collective-permute-start(f32[4,16,256]{2,1,0:T(8,128)S(1)} %copy-done.28), channel_id=1, source_target_pairs={{0,16},{8,24},{16,0},{24,8},{1,17},{9,25},{17,1},{25,9},{2,18},{10... | collective-permute-start | bytes 196616 | tf_op jit(solution)/shard_map/ppermute | solution.py:320
  54.9 7.3 %collective-permute-start.26 = (f32[4,16,256]{2,1,0:T(8,128)S(1)}, f32[4,16,256]{2,1,0:T(8,128)S(1)}, u32[]{:S(2)}, u32[]{:S(2)}) collective-permute-start(f32[4,16,256]{2,1,0:T(8,128)S(1)} %copy-done.27), channel_id=1, source_target_pairs={{0,24},{8,16},{16,8},{24,0},{1,25},{9,17},{17,9},{25,1},{2,26},{10... | collective-permute-start | bytes 196616 | tf_op jit(solution)/shard_map/ppermute | solution.py:320
  55.9 9.7 %collective-permute-start.12 = (f32[4,16,256]{2,1,0:T(8,128)}, f32[4,16,256]{2,1,0:T(8,128)S(1)}, u32[]{:S(2)}, u32[]{:S(2)}) collective-permute-start(f32[4,16,256]{2,1,0:T(8,128)} %get-tuple-element.63), channel_id=1, source_target_pairs={{0,8},{8,0},{16,24},{24,16},{1,9},{9,1},{17,25},{25,17},{2,10},{10... | collective-permute-start | bytes 196616 | tf_op jit(solution)/shard_map/ppermute | solution.py:320
  58.7 23.9 %copy-start.14 = (f32[4,16,256]{2,1,0:T(8,128)}, f32[4,16,256]{2,1,0:T(8,128)S(1)}, u32[]{:S(2)}) copy-start(f32[4,16,256]{2,1,0:T(8,128)S(1)} %collective-permute-done.6.refs_5_) | copy-start | bytes 196612
  58.7 9.6 %collective-permute-start.13 = (f32[4,16,256]{2,1,0:T(8,128)}, f32[4,16,256]{2,1,0:T(8,128)S(1)}, u32[]{:S(2)}, u32[]{:S(2)}) collective-permute-start(f32[4,16,256]{2,1,0:T(8,128)} %get-tuple-element.64), channel_id=1, source_target_pairs={{0,16},{8,24},{16,0},{24,8},{1,17},{9,25},{17,1},{25,9},{2,18},{10... | collective-permute-start | bytes 196616 | tf_op jit(solution)/shard_map/ppermute | solution.py:320
  61.2 17.4 %copy-start.5 = (f32[4,16,256]{2,1,0:T(8,128)}, f32[4,16,256]{2,1,0:T(8,128)S(1)}, u32[]{:S(2)}) copy-start(f32[4,16,256]{2,1,0:T(8,128)S(1)} %collective-permute-done.24.refs_5_) | copy-start | bytes 196612
  61.2 7.7 %collective-permute-start.14 = (f32[4,16,256]{2,1,0:T(8,128)}, f32[4,16,256]{2,1,0:T(8,128)S(1)}, u32[]{:S(2)}, u32[]{:S(2)}) collective-permute-start(f32[4,16,256]{2,1,0:T(8,128)} %get-tuple-element.65), channel_id=1, source_target_pairs={{0,24},{8,16},{16,8},{24,0},{1,25},{9,17},{17,9},{25,1},{2,26},{10... | collective-permute-start | bytes 196616 | tf_op jit(solution)/shard_map/ppermute | solution.py:320
  62.2 16.5 %copy-start.6 = (f32[4,16,256]{2,1,0:T(8,128)}, f32[4,16,256]{2,1,0:T(8,128)S(1)}, u32[]{:S(2)}) copy-start(f32[4,16,256]{2,1,0:T(8,128)S(1)} %collective-permute-done.25.refs_6_) | copy-start | bytes 196612
  62.2 9.2 %collective-permute-start.21 = (f32[4,16,256]{2,1,0:T(8,128)}, f32[4,16,256]{2,1,0:T(8,128)S(1)}, u32[]{:S(2)}, u32[]{:S(2)}) collective-permute-start(f32[4,16,256]{2,1,0:T(8,128)} %get-tuple-element.76), channel_id=1, source_target_pairs={{0,8},{8,0},{16,24},{24,16},{1,9},{9,1},{17,25},{25,17},{2,10},{10... | collective-permute-start | bytes 196616 | tf_op jit(solution)/shard_map/ppermute | solution.py:320
  62.2 16.5 %copy-start.7 = (f32[4,16,256]{2,1,0:T(8,128)}, f32[4,16,256]{2,1,0:T(8,128)S(1)}, u32[]{:S(2)}) copy-start(f32[4,16,256]{2,1,0:T(8,128)S(1)} %collective-permute-done.26.refs_7_) | copy-start | bytes 196612
  62.2 13.9 %collective-permute-start.22 = (f32[4,16,256]{2,1,0:T(8,128)}, f32[4,16,256]{2,1,0:T(8,128)S(1)}, u32[]{:S(2)}, u32[]{:S(2)}) collective-permute-start(f32[4,16,256]{2,1,0:T(8,128)} %get-tuple-element.77), channel_id=1, source_target_pairs={{0,16},{8,24},{16,0},{24,8},{1,17},{9,25},{17,1},{25,9},{2,18},{10... | collective-permute-start | bytes 196616 | tf_op jit(solution)/shard_map/ppermute | solution.py:320
  65.6 14.9 %copy-start.15 = (f32[4,16,256]{2,1,0:T(8,128)}, f32[4,16,256]{2,1,0:T(8,128)S(1)}, u32[]{:S(2)}) copy-start(f32[4,16,256]{2,1,0:T(8,128)S(1)} %collective-permute-done.12.refs_1_) | copy-start | bytes 196612
  65.6 10.5 %collective-permute-start.23 = (f32[4,16,256]{2,1,0:T(8,128)}, f32[4,16,256]{2,1,0:T(8,128)S(1)}, u32[]{:S(2)}, u32[]{:S(2)}) collective-permute-start(f32[4,16,256]{2,1,0:T(8,128)} %get-tuple-element.78), channel_id=1, source_target_pairs={{0,24},{8,16},{16,8},{24,0},{1,25},{9,17},{17,9},{25,1},{2,26},{10... | collective-permute-start | bytes 196616 | tf_op jit(solution)/shard_map/ppermute | solution.py:320
  68.3 12.3 %copy-start.16 = (f32[4,16,256]{2,1,0:T(8,128)}, f32[4,16,256]{2,1,0:T(8,128)S(1)}, u32[]{:S(2)}) copy-start(f32[4,16,256]{2,1,0:T(8,128)S(1)} %collective-permute-done.13.refs_2_) | copy-start | bytes 196612
  68.3 14.1 %collective-permute-start.7 = (f32[4,16,256]{2,1,0:T(8,128)}, f32[4,16,256]{2,1,0:T(8,128)S(1)}, u32[]{:S(2)}, u32[]{:S(2)}) collective-permute-start(f32[4,16,256]{2,1,0:T(8,128)} %get-tuple-element.55), channel_id=1, source_target_pairs={{0,16},{8,24},{16,0},{24,8},{1,17},{9,25},{17,1},{25,9},{2,18},{10... | collective-permute-start | bytes 196616 | tf_op jit(solution)/shard_map/ppermute | solution.py:320
  69.0 11.6 %copy-start.17 = (f32[4,16,256]{2,1,0:T(8,128)}, f32[4,16,256]{2,1,0:T(8,128)S(1)}, u32[]{:S(2)}) copy-start(f32[4,16,256]{2,1,0:T(8,128)S(1)} %collective-permute-done.14.refs_3_) | copy-start | bytes 196612
  69.0 13.4 %collective-permute-start.8 = (f32[4,16,256]{2,1,0:T(8,128)}, f32[4,16,256]{2,1,0:T(8,128)S(1)}, u32[]{:S(2)}, u32[]{:S(2)}) collective-permute-start(f32[4,16,256]{2,1,0:T(8,128)} %get-tuple-element.56), channel_id=1, source_target_pairs={{0,24},{8,16},{16,8},{24,0},{1,25},{9,17},{17,9},{25,1},{2,26},{10... | collective-permute-start | bytes 196616 | tf_op jit(solution)/shard_map/ppermute | solution.py:320
  71.3 7.3 %copy-start.8 = (f32[4,16,256]{2,1,0:T(8,128)}, f32[4,16,256]{2,1,0:T(8,128)S(1)}, u32[]{:S(2)}) copy-start(f32[4,16,256]{2,1,0:T(8,128)S(1)} %collective-permute-done.21.refs_1_) | copy-start | bytes 196612
  71.3 11.1 %collective-permute-start.3 = (f32[4,16,256]{2,1,0:T(8,128)}, f32[4,16,256]{2,1,0:T(8,128)S(1)}, u32[]{:S(2)}, u32[]{:S(2)}) collective-permute-start(f32[4,16,256]{2,1,0:T(8,128)} %get-tuple-element.50), channel_id=1, source_target_pairs={{0,8},{8,0},{16,24},{24,16},{1,9},{9,1},{17,25},{25,17},{2,10},{10... | collective-permute-start | bytes 196616 | tf_op jit(solution)/shard_map/ppermute | solution.py:320
  76.1 6.3 %collective-permute-start.4 = (f32[4,16,256]{2,1,0:T(8,128)}, f32[4,16,256]{2,1,0:T(8,128)S(1)}, u32[]{:S(2)}, u32[]{:S(2)}) collective-permute-start(f32[4,16,256]{2,1,0:T(8,128)} %get-tuple-element.51), channel_id=1, source_target_pairs={{0,16},{8,24},{16,0},{24,8},{1,17},{9,25},{17,1},{25,9},{2,18},{10... | collective-permute-start | bytes 196616 | tf_op jit(solution)/shard_map/ppermute | solution.py:320
  76.2 6.4 %collective-permute-start.5 = (f32[4,16,256]{2,1,0:T(8,128)}, f32[4,16,256]{2,1,0:T(8,128)S(1)}, u32[]{:S(2)}, u32[]{:S(2)}) collective-permute-start(f32[4,16,256]{2,1,0:T(8,128)} %get-tuple-element.52), channel_id=1, source_target_pairs={{0,24},{8,16},{16,8},{24,0},{1,25},{9,17},{17,9},{25,1},{2,26},{10... | collective-permute-start | bytes 196616 | tf_op jit(solution)/shard_map/ppermute | solution.py:320
  (10 other events, 11.9 us)

commit v2 on v1

v2 whole, which is shorter than its diff:
```python
import functools
import math
import jax
import jax.numpy as jnp
from jax import lax
from jax.experimental import pallas as pl
from jax.experimental.pallas import tpu as pltpu
from jax.sharding import PartitionSpec as P

MARGIN = 16
JIT = 8
VIEWS = 3

SHEAR_ROWS = (0.75, -0.5, 0.25)
SHEAR_COLS = (-0.25, 0.625, -0.875)

TILE = 8
GRID = 32
BF = jnp.bfloat16
F32 = jnp.float32
SMEM = pl.BlockSpec(memory_space=pltpu.SMEM)
VMEM = pl.BlockSpec(memory_space=pltpu.VMEM)
ANY = pl.BlockSpec(memory_space=pl.ANY)


def near(shape):
    return pltpu.VMEM(shape, F32)


def held(*arrays):
    return [pltpu.with_memory_space_constraint(array, pltpu.VMEM) for array in arrays]


def shared_spill(view, slices, phases):
    reach = abs(SHEAR_ROWS[view]) * (MARGIN - 2) * (slices - 1) / slices + JIT + 1
    need = -(-(math.ceil(reach) - 1) // phases)
    assert need <= TILE and phases & (phases - 1) == 0
    return 2 * need <= TILE


def canvas_rows(view, slices, phases, length):
    return length + (1 if shared_spill(view, slices, phases) else 2) * TILE * phases


def render_kernel(view, phases, offs, order, dens, emis, home, rim, dbuf, ebuf, drow, dcol, hs, rs, sem):
    slices, length, columns = dens.shape
    bricks = columns // length
    half = length // 2
    quota = length // phases
    back = order[0, view] == 1

    def slice_at(k):
        return jnp.where(back, slices - 1 - k, k)

    def copies(z):
        return (
            pltpu.make_async_copy(dens.at[z], dbuf.at[z], sem.at[0, z]),
            pltpu.make_async_copy(emis.at[:, z], ebuf.at[:, z], sem.at[1, z]),
        )

    for k in range(slices):
        for copy in copies(slice_at(k)):
            copy.start()

    def row_table(count, place):
        shape = (phases, count, length)
        phase = lax.broadcasted_iota(jnp.int32, shape, 0)
        spot = lax.broadcasted_iota(jnp.int32, shape, 1)
        source = lax.broadcasted_iota(jnp.int32, shape, 2)
        table = place(spot) * phases + phase - source
        return table.astype(F32).reshape(phases * count, length).astype(BF)

    spill = TILE * phases
    drow[0:length] = row_table(quota, lambda spot: spot)
    if drow.shape[0] == length + spill:
        drow[length:] = row_table(
            TILE, lambda spot: jnp.where(spot < TILE // 2, spot + quota, spot - TILE)
        )
    else:
        drow[length : length + spill] = row_table(TILE, lambda spot: spot - TILE)
        drow[length + spill :] = row_table(TILE, lambda spot: spot + quota)
    lane = lax.broadcasted_iota(jnp.int32, (length, length), 1)
    source = lax.broadcasted_iota(jnp.int32, (length, length), 0)
    dcol[0] = (lane - source).astype(F32).astype(BF)
    dcol[1] = (jnp.where(lane < half, lane + length, lane - length) - source).astype(F32).astype(BF)
    dcol[2] = (jnp.where(lane < half, lane - half, lane + half) - source).astype(F32).astype(BF)
    for ref in (home, rim):
        ref[0:3] = jnp.zeros((3,) + ref.shape[1:], F32)
        ref[3] = jnp.ones(ref.shape[1:], F32)

    def bilinear(distance, offset, rate, z):
        grid_rate = rate * (MARGIN - 2) * GRID / slices
        assert grid_rate == int(grid_rate)
        shift = offset * GRID + (2 * z - (slices - 1)) * int(grid_rate)
        whole = shift >> (GRID.bit_length() - 1)
        rest = (shift & (GRID - 1)).astype(F32) * (1.0 / GRID)
        near = (distance - whole.astype(F32).astype(BF)) - rest.astype(BF)
        one = jnp.ones((), BF)
        return jnp.maximum(one - jnp.abs(near), jnp.zeros((), BF))

    def resample(k, slot):
        z = slice_at(k)
        for copy in copies(z):
            copy.wait()
        for b in range(bricks):
            part = slice(b * length, (b + 1) * length)
            distance = jnp.concatenate([dcol[0], dcol[1 + b]], 1)
            weights = bilinear(distance, offs[1, 0, 0, b, view], SHEAR_COLS[view], z)
            cells = jnp.concatenate([dbuf[z, :, part]] + [ebuf[c, z, :, part] for c in range(3)], 0)
            resampled = jnp.dot(cells, weights, preferred_element_type=F32).astype(BF)
            for f in range(4):
                field = slice(f * length, (f + 1) * length)
                hs[slot, b, :, field] = resampled[field, :length]
                rs[slot, part, field] = resampled[field, length:]

    def shade(footprint, ref, part):
        through = ref[3, :, part]
        passed = through * jnp.exp(-footprint[:, :length])
        weight = through - passed
        ref[3, :, part] = passed
        for c in range(3):
            color = footprint[:, (c + 1) * length : (c + 2) * length]
            ref[c, :, part] = ref[c, :, part] + color * weight

    def deposit(k, slot):
        z = slice_at(k)
        weights = [
            bilinear(drow[...], offs[0, 0, 0, b, view], SHEAR_ROWS[view], z) for b in range(bricks)
        ]
        for b in range(bricks):
            shade(
                jnp.dot(weights[b], hs[slot, b], preferred_element_type=F32),
                home,
                slice(b * length, (b + 1) * length),
            )
        both = jnp.concatenate(weights, 1)
        shade(jnp.dot(both, rs[slot], preferred_element_type=F32), rim, slice(0, length))

    resample(0, 0)

    def step(pair, carry):
        k = 2 * pair
        resample(k + 1, 1)
        deposit(k, 0)
        resample(k + 2, 0)
        deposit(k + 1, 1)
        return carry

    assert slices % 2 == 0
    lax.fori_loop(0, slices // 2 - 1, step, 0)
    resample(slices - 1, 1)
    deposit(slices - 2, 0)
    deposit(slices - 1, 1)


def render(view, phases, offsets, orders, density, emission):
    slices, length, columns = density.shape
    rows = canvas_rows(view, slices, phases, length)
    bricks = columns // length
    assert bricks == 2 and length == 128
    return pl.pallas_call(
        functools.partial(render_kernel, view, phases),
        out_shape=(near((4, rows, columns)), near((4, rows, length))),
        in_specs=[SMEM, SMEM, ANY, ANY],
        out_specs=(VMEM, VMEM),
        scratch_shapes=[
            pltpu.VMEM(density.shape, BF),
            pltpu.VMEM(emission.shape, BF),
            pltpu.VMEM((rows, length), BF),
            pltpu.VMEM((3, length, length), BF),
            pltpu.VMEM((2, bricks, length, 4 * length), BF),
            pltpu.VMEM((2, bricks * length, 4 * length), BF),
            pltpu.SemaphoreType.DMA((2, slices)),
        ],
        compiler_params=pltpu.CompilerParams(vmem_limit_bytes=16 << 20),
        name=f"render{view}",
    )(offsets, orders, *(pltpu.with_memory_space_constraint(array, pltpu.HBM) for array in (density, emission)))


def joined(channel, one, other):
    return one * other if channel == 3 else one + other


def fold_kernel(shared, phases, home, rim, low, high, canvas, up, down):
    columns = home.shape[2]
    lanes = columns // 2
    half, quarter = lanes // 2, lanes // 4
    quota = canvas.shape[2]
    length = quota * phases

    def folded(c, start, count):
        part = pl.ds(start, count)
        lane = lax.broadcasted_iota(jnp.int32, (count, lanes), 1)
        neutral = 1.0 if c == 3 else 0.0
        own = rim[c, part]
        first = jnp.where(lane < half, own, low[c, part])
        first = jnp.where((lane >= quarter) & (lane < lanes - quarter), first, neutral)
        second = jnp.where(lane < half, own, high[c, part])
        second = jnp.where((lane < quarter) | (lane >= lanes - quarter), second, neutral)
        return (
            joined(c, home[c, part, 0:lanes], pltpu.roll(first, half, 1)),
            joined(c, home[c, part, lanes:columns], second),
        )

    for c in range(4):
        for p in range(phases):
            one, other = folded(c, p * quota, quota)
            canvas[c, p, :, 0:lanes] = one
            canvas[c, p, :, lanes:columns] = other
        if shared:
            sub = lax.broadcasted_iota(jnp.int32, (TILE, lanes), 0)
            for j in range(phases // 2):
                one = folded(c, length + 2 * j * TILE, TILE)
                other = folded(c, length + (2 * j + 1) * TILE, TILE)
                for n in range(2):
                    turned = pltpu.roll(other[n], TILE // 2, 0)
                    part = slice(n * lanes, (n + 1) * lanes)
                    up[c, j, :, part] = jnp.where(sub < TILE // 2, turned, one[n])
                    down[c, j, :, part] = jnp.where(sub < TILE // 2, one[n], turned)
        else:
            for p in range(phases):
                for n, out in enumerate((up, down)):
                    one, other = folded(c, length + (n * phases + p) * TILE, TILE)
                    out[c, p, :, 0:lanes] = one
                    out[c, p, :, lanes:columns] = other


def fold(view, slices, length, phases, home, rim, low, high):
    columns = home.shape[2]
    shared = shared_spill(view, slices, phases)
    packs = phases // 2 if shared else phases
    return pl.pallas_call(
        functools.partial(fold_kernel, shared, phases),
        out_shape=(
            near((4, phases, length // phases, columns)),
            near((4, packs, TILE, columns)),
            near((4, packs, TILE, columns)),
        ),
        in_specs=[VMEM] * 4,
        out_specs=(VMEM,) * 3,
        compiler_params=pltpu.CompilerParams(vmem_limit_bytes=4 << 20),
        name=f"fold{view}",
    )(*held(home, rim, low, high))


def finish_kernel(shared, canvas, above, below, kept, given):
    me = lax.axis_index("depth")
    bit = me & 1
    quota = canvas.shape[2]
    for n in range(kept.shape[1]):
        for out, odd in ((kept, bit), (given, 1 - bit)):
            p = 2 * n + odd
            for c in range(4):
                if shared:
                    neutral = 1.0 if c == 3 else 0.0
                    sub = lax.broadcasted_iota(jnp.int32, above.shape[2:], 0)
                    top, bottom = above[c, n], below[c, n]
                    top = jnp.where(odd == 1, pltpu.roll(top, TILE // 2, 0), top)
                    bottom = jnp.where(odd == 1, pltpu.roll(bottom, TILE // 2, 0), bottom)
                    top = jnp.where(sub < TILE // 2, top, neutral)
                    bottom = jnp.where(sub < TILE // 2, neutral, bottom)
                else:
                    top, bottom = above[c, p], below[c, p]
                out[c, n, 0:TILE] = joined(c, canvas[c, p, 0:TILE], top)
                if quota > 2 * TILE:
                    out[c, n, TILE : quota - TILE] = canvas[c, p, TILE : quota - TILE]
                out[c, n, quota - TILE :] = joined(c, canvas[c, p, quota - TILE :], bottom)


def finish(view, shared, canvas, above, below):
    channels, phases, quota, columns = canvas.shape
    return pl.pallas_call(
        functools.partial(finish_kernel, shared),
        out_shape=(near((channels, phases // 2, quota, columns)),) * 2,
        in_specs=[VMEM] * 3,
        out_specs=(VMEM,) * 2,
        compiler_params=pltpu.CompilerParams(vmem_limit_bytes=4 << 20),
        name=f"finish{view}",
    )(*held(canvas, above, below))


def over(own_first, own, other):
    front = [jnp.where(own_first, a, b) for a, b in zip(own, other)]
    rear = [jnp.where(own_first, b, a) for a, b in zip(own, other)]
    return [f + front[3] * r for f, r in zip(front[:3], rear[:3])] + [front[3] * rear[3]]


def own_first(view, level, order):
    me = lax.axis_index("depth")
    return jnp.logical_xor((me >> level & 1) == 0, order[0, view] == 1)


def merge_kernel(view, level, order, kept, received, next_kept, next_given):
    ahead = own_first(view, level, order)
    bit = lax.axis_index("depth") >> (level + 1) & 1
    for n in range(next_kept.shape[1]):
        for out, odd in ((next_kept, bit), (next_given, 1 - bit)):
            p = 2 * n + odd
            pixels = over(ahead, [kept[c, p] for c in range(4)], [received[c, p] for c in range(4)])
            for c in range(4):
                out[c, n] = pixels[c]


def merge(view, level, orders, kept, received):
    channels, phases, quota, columns = kept.shape
    return pl.pallas_call(
        functools.partial(merge_kernel, view, level),
        out_shape=(near((channels, phases // 2, quota, columns)),) * 2,
        in_specs=[SMEM] + [VMEM] * 2,
        out_specs=(VMEM,) * 2,
        compiler_params=pltpu.CompilerParams(vmem_limit_bytes=4 << 20),
        name=f"merge{view}_{level}",
    )(orders, *held(kept, received))


def emit_kernel(view, level, order, kept, received, *refs):
    out, stage, sem = refs[-3:]
    ahead = own_first(view, level, order)
    quota, columns = kept.shape[2:]
    lanes = stage.shape[2]
    pieces = columns // lanes
    pixels = over(ahead, [kept[c, 0] for c in range(4)], [received[c, 0] for c in range(4)])
    for c in range(4):
        for n in range(pieces):
            stage[c, pl.ds(n, quota, stride=pieces), :] = pixels[c][:, n * lanes : (n + 1) * lanes]
    copy = pltpu.make_async_copy(stage, out.at[view], sem)
    copy.start()
    copy.wait()


def emit(view, level, orders, kept, received, image):
    channels, _, quota, columns = kept.shape
    shape = (channels, quota * columns // 128, 128)
    operands = [orders, *held(kept, received)]
    specs = [SMEM, VMEM, VMEM]
    aliases = {}
    if image is not None:
        operands.append(image)
        specs.append(ANY)
        aliases = {3: 0}
    return pl.pallas_call(
        functools.partial(emit_kernel, view, level),
        out_shape=jax.ShapeDtypeStruct((VIEWS,) + shape, F32),
        in_specs=specs,
        out_specs=ANY,
        scratch_shapes=[pltpu.VMEM(shape, F32), pltpu.SemaphoreType.DMA],
        input_output_aliases=aliases,
        compiler_params=pltpu.CompilerParams(vmem_limit_bytes=4 << 20),
        name=f"emit{view}",
    )(*operands)


def shifted(block, axis, step):
    count = lax.axis_size(axis)
    return lax.ppermute(block, axis, [(i, (i + step) % count) for i in range(count)])


def swapped(block, level):
    count = lax.axis_size("depth")
    return lax.ppermute(block, "depth", [(i, i ^ 1 << level) for i in range(count)])


def local(density, emission, offsets, view_order):
    slices, length, columns = density.shape
    phases = lax.axis_size("depth")
    levels = phases.bit_length() - 1
    offsets = offsets.transpose(1, 2, 3, 4, 0)
    orders = view_order.transpose(1, 0)
    image = None
    for view in range(VIEWS):
        shared = shared_spill(view, slices, phases)
        home, rim = render(view, phases, offsets, orders, density, emission)
        low = shifted(rim, "col", 1)
        high = low if lax.axis_size("col") == 2 else shifted(rim, "col", -1)
        canvas, up, down = fold(view, slices, length, phases, home, rim, low, high)
        above = shifted(down, "row", 1)
        below = shifted(up, "row", -1)
        kept, given = finish(view, shared, canvas, above, below)
        for level in range(levels - 1):
            kept, given = merge(view, level, orders, kept, swapped(given, level))
        image = emit(view, levels - 1, orders, kept, swapped(given, levels - 1), image)
    return image.reshape(VIEWS, 4, length // phases, 1, columns)


def solution(mesh):
    return jax.shard_map(
        local,
        mesh=mesh,
        in_specs=(
            P("depth", "row", "col"),
            P(None, "depth", "row", "col"),
            P(None, None, "depth", "row", "col"),
            P(None, "row"),
        ),
        out_specs=P(None, None, "row", "depth", "col"),
        check_vma=False,
    )
```

time: 87.8 us -> 67.6 us (0.77)
  waiting for transfers between devices: 0.92 us -> 25.8 us
  starting transfers between devices: 39.8 us -> 18.1 us
  Pallas kernels: 39.8 us -> 22 us
  local copies, waits for them, and re-layouts: 6.29 us -> 1.41 us
    ppermute x18 -> x6, starting transfers between devices: 29.2 us -> 7.84 us  [swapped(): lax.ppermute(block, 'depth', [(i, i ^ 1 << level) for i in range(count)])]
    ppermute x18 -> x6, waiting for transfers between devices: 0.9 us -> 21.1 us  [swapped(): lax.ppermute(block, 'depth', [(i, i ^ 1 << level) for i in range(count)])]
    pallas_call x3, Pallas kernels: 7.28 us -> 0.51 us  [fold(): pl.pallas_call(functools.partial(fold_kernel, shared, phases), out_shape=...]
    pallas_call x3, Pallas kernels: 21.9 us -> 15.8 us  [render(): pl.pallas_call(functools.partial(render_kernel, view, phases), out_shape=...]
    pallas_call x6 -> x9, Pallas kernels: 10.6 us -> 5.64 us  [the longest x3 3.7 us: emit(): pl.pallas_call(functools.partial(emit_kernel, view, level), out_shape=jax...]
    ppermute x9, waiting for transfers between devices: 0.02 us -> 4.67 us  [shifted(): lax.ppermute(block, axis, [(i, (i + step) % count) for i in range(count)])]
    unnamed x64 -> x8, local copies, waits for them, and re-layouts: 4.15 us -> 1.41 us
    broadcast_in_dim x1 -> x0, local copies, waits for them, and re-layouts: 2.15 us -> none  [local(): return image[:, :, :, None, :]]
  transfers between devices with their start and end apart: 27 -> 15, of which waited for: 2 -> 7; matrix products, arithmetic and copies ran while one was open for 0% -> 0% of each run, Pallas kernels for 35% -> 23%
where the time goes in v2:
time: 67.6 us; the launch traced here: 67.4 us
  waiting for transfers between devices  25.8 us (38%)
  Pallas kernels  22 us (33%)
  starting transfers between devices  18.1 us (27%)
  local copies, waits for them, and re-layouts  1.41 us (2%)
    ppermute x6, waiting for transfers between devices, swapped(): lax.ppermute(block, 'depth', [(i, i ^ 1 << level) for i in range(count)])  21.1 us
    pallas_call x3, Pallas kernels, render(): pl.pallas_call(functools.partial(render_kernel, view, phases), out_shape=...  15.8 us
    ppermute x9, starting transfers between devices, shifted(): lax.ppermute(block, axis, [(i, (i + step) % count) for i in range(count)])  10.3 us
    ppermute x6, starting transfers between devices, swapped(): lax.ppermute(block, 'depth', [(i, i ^ 1 << level) for i in range(count)])  7.84 us
    ppermute x9, waiting for transfers between devices, shifted(): lax.ppermute(block, axis, [(i, (i + step) % count) for i in range(count)])  4.67 us
    pallas_call x3, Pallas kernels, emit(): pl.pallas_call(functools.partial(emit_kernel, view, level), out_shape=jax...  3.7 us
    pallas_call x3, Pallas kernels, merge(): pl.pallas_call(functools.partial(merge_kernel, view, level), out_shape=(n...  1.8 us
    unnamed x8, local copies, waits for them, and re-layouts  1.41 us
  transfers between devices with their start and end apart: 15, of which 7 were waited for; matrix products, arithmetic and copies ran while one was open for 0% of the time, Pallas kernels for 23%

profile of v2, /device:TPU:0, one launch (start us, length us, event | category | flops | bytes accessed | tf_op | source)
XLA Modules:
  0.0 67.4 jit_solution(12500847134292772167)
XLA Ops:
  0.0 0.0 copy-start.1
  0.0 0.7 %copy-done = s32[3,1]{0,1:T(1,128)S(1)} copy-done((s32[3,1]{0,1:T(1,128)S(1)}, s32[3,1]{0,1:T(1,128)}, u32[]{:S(2)}) %copy-start) | copy-done | bytes 36
  0.7 0.7 %copy-done.2 = s32[3,2,1,1,2]{0,4,3,2,1:T(2,128)S(1)} copy-done((s32[3,2,1,1,2]{0,4,3,2,1:T(2,128)S(1)}, s32[3,2,1,1,2]{0,4,3,2,1:T(2,128)}, u32[]{:S(2)}) %copy-start.2) | copy-done | bytes 72
  1.4 5.4 %render0.1 = (f32[4,192,256]{2,1,0:T(8,128)S(1)}, f32[4,192,128]{2,1,0:T(8,128)S(1)}) custom-call(s32[2,1,1,2,3]{4,3,2,1,0:T(2,128)S(1)} %bitcast.12, s32[1,3]{1,0:T(1,128)S(1)} %bitcast.3, bf16[8,128,256]{2,1,0:T(8,128)(2,1)} %dens.5, bf16[3,8,128,256]{3,2,1,0:T(8,128)(2,1)} %emis.5), custom_call_target="tpu_custom_call" | custom-call | tf_op jit(solution)/shard_map/render0/pallas_call | solution.py:161
  6.8 0.6 collective-permute-start.10
  7.4 0.0 copy-done.1
  7.4 0.0 copy-done.3
  7.4 5.2 %render1.1 = (f32[4,160,256]{2,1,0:T(8,128)S(1)}, f32[4,160,128]{2,1,0:T(8,128)S(1)}) custom-call(s32[2,1,1,2,3]{4,3,2,1,0:T(2,128)S(1)} %bitcast.13, s32[1,3]{1,0:T(1,128)S(1)} %bitcast.4, bf16[8,128,256]{2,1,0:T(8,128)(2,1)} %dens.5, bf16[3,8,128,256]{3,2,1,0:T(8,128)(2,1)} %emis.5), custom_call_target="tpu_custom_call" | custom-call | tf_op jit(solution)/shard_map/render1/pallas_call | solution.py:161
  12.6 0.1 collective-permute-start.5
  12.7 5.2 %render2.1 = (f32[4,160,256]{2,1,0:T(8,128)S(1)}, f32[4,160,128]{2,1,0:T(8,128)S(1)}) custom-call(s32[2,1,1,2,3]{4,3,2,1,0:T(2,128)S(1)} %bitcast.14, s32[1,3]{1,0:T(1,128)S(1)} %bitcast.5, bf16[8,128,256]{2,1,0:T(8,128)(2,1)} %dens.5, bf16[3,8,128,256]{3,2,1,0:T(8,128)(2,1)} %emis.5), custom_call_target="tpu_custom_call" | custom-call | tf_op jit(solution)/shard_map/render2/pallas_call | solution.py:161
  17.9 0.5 collective-permute-start
  18.5 0.0 collective-permute-done.10.low.high
  18.5 0.2 fold0.1
  18.6 2.6 %collective-permute-start.11 = (f32[4,4,8,256]{3,2,1,0:T(8,128)S(1)}, f32[4,4,8,256]{3,2,1,0:T(8,128)S(1)}, u32[]{:S(2)}, u32[]{:S(2)}) collective-permute-start(f32[4,4,8,256]{3,2,1,0:T(8,128)S(1)} %get-tuple-element.53), channel_id=1, source_target_pairs={{0,2},{2,4},{4,6},{6,0},{1,3},{3,5},{5,7},{7,1},{8,10},{10,12},{12... | collective-permute-start | bytes 393224 | tf_op jit(solution)/shard_map/ppermute | solution.py:355
  21.2 1.0 %collective-permute-start.12 = (f32[4,4,8,256]{3,2,1,0:T(8,128)S(1)}, f32[4,4,8,256]{3,2,1,0:T(8,128)S(1)}, u32[]{:S(2)}, u32[]{:S(2)}) collective-permute-start(f32[4,4,8,256]{3,2,1,0:T(8,128)S(1)} %get-tuple-element.54), channel_id=1, source_target_pairs={{0,6},{2,0},{4,2},{6,4},{1,7},{3,1},{5,3},{7,5},{8,14},{10,8},{12,... | collective-permute-start | bytes 393224 | tf_op jit(solution)/shard_map/ppermute | solution.py:355
  22.2 0.0 collective-permute-done.5.low.high
  22.2 0.2 fold1.1
  22.4 1.1 %collective-permute-start.6 = (f32[4,2,8,256]{3,2,1,0:T(8,128)S(1)}, f32[4,2,8,256]{3,2,1,0:T(8,128)S(1)}, u32[]{:S(2)}, u32[]{:S(2)}) collective-permute-start(f32[4,2,8,256]{3,2,1,0:T(8,128)S(1)} %get-tuple-element.44), channel_id=1, source_target_pairs={{0,2},{2,4},{4,6},{6,0},{1,3},{3,5},{5,7},{7,1},{8,10},{10,12},{12... | collective-permute-start | bytes 196616 | tf_op jit(solution)/shard_map/ppermute | solution.py:355
  23.4 1.9 %collective-permute-start.7 = (f32[4,2,8,256]{3,2,1,0:T(8,128)S(1)}, f32[4,2,8,256]{3,2,1,0:T(8,128)S(1)}, u32[]{:S(2)}, u32[]{:S(2)}) collective-permute-start(f32[4,2,8,256]{3,2,1,0:T(8,128)S(1)} %get-tuple-element.45), channel_id=1, source_target_pairs={{0,6},{2,0},{4,2},{6,4},{1,7},{3,1},{5,3},{7,5},{8,14},{10,8},{12,... | collective-permute-start | bytes 196616 | tf_op jit(solution)/shard_map/ppermute | solution.py:355
  25.4 0.0 collective-permute-done.low.high
  25.4 0.2 fold2.1
  25.5 0.5 collective-permute-start.1
  26.1 4.6 %collective-permute-done.6.above = f32[4,2,8,256]{3,2,1,0:T(8,128)S(1)} collective-permute-done((f32[4,2,8,256]{3,2,1,0:T(8,128)S(1)}, f32[4,2,8,256]{3,2,1,0:T(8,128)S(1)}, u32[]{:S(2)}, u32[]{:S(2)}) %collective-permute-start.6) | collective-permute-done | bytes 65568 | tf_op jit(solution)/shard_map/ppermute | solution.py:355
  30.7 2.0 %collective-permute-start.2 = (f32[4,2,8,256]{3,2,1,0:T(8,128)S(1)}, f32[4,2,8,256]{3,2,1,0:T(8,128)S(1)}, u32[]{:S(2)}, u32[]{:S(2)}) collective-permute-start(f32[4,2,8,256]{3,2,1,0:T(8,128)S(1)} %get-tuple-element.36), channel_id=1, source_target_pairs={{0,6},{2,0},{4,2},{6,4},{1,7},{3,1},{5,3},{7,5},{8,14},{10,8},{12,... | collective-permute-start | bytes 196616 | tf_op jit(solution)/shard_map/ppermute | solution.py:355
  32.7 0.0 collective-permute-done.7.below
  32.8 1.6 %collective-permute-start.8 = (f32[4,2,32,256]{3,2,1,0:T(8,128)S(1)}, f32[4,2,32,256]{3,2,1,0:T(8,128)S(1)}, u32[]{:S(2)}, u32[]{:S(2)}) collective-permute-start(f32[4,2,32,256]{3,2,1,0:T(8,128)S(1)} %get-tuple-element.47), channel_id=1, source_target_pairs={{0,8},{8,0},{16,24},{24,16},{1,9},{9,1},{17,25},{25,17},{2,10},{10... | collective-permute-start | bytes 786440 | tf_op jit(solution)/shard_map/ppermute | solution.py:360
  34.4 0.0 collective-permute-done.11.above
  34.4 0.0 collective-permute-done.12.below
  34.4 0.1 finish0.1
  34.5 0.5 collective-permute-start.13
  35.0 0.0 collective-permute-done.1.above
  35.0 0.0 collective-permute-done.2.below
  35.1 2.1 %collective-permute-start.3 = (f32[4,2,32,256]{3,2,1,0:T(8,128)S(1)}, f32[4,2,32,256]{3,2,1,0:T(8,128)S(1)}, u32[]{:S(2)}, u32[]{:S(2)}) collective-permute-start(f32[4,2,32,256]{3,2,1,0:T(8,128)S(1)} %get-tuple-element.38), channel_id=1, source_target_pairs={{0,8},{8,0},{16,24},{24,16},{1,9},{9,1},{17,25},{25,17},{2,10},{10... | collective-permute-start | bytes 786440 | tf_op jit(solution)/shard_map/ppermute | solution.py:360
  37.1 4.9 %collective-permute-done.8.received = f32[4,2,32,256]{3,2,1,0:T(8,128)S(1)} collective-permute-done((f32[4,2,32,256]{3,2,1,0:T(8,128)S(1)}, f32[4,2,32,256]{3,2,1,0:T(8,128)S(1)}, u32[]{:S(2)}, u32[]{:S(2)}) %collective-permute-start.8) | collective-permute-done | bytes 262176 | tf_op jit(solution)/shard_map/ppermute | solution.py:360
  42.0 0.6 merge1_0.1
  42.6 5.0 %collective-permute-done.13.received = f32[4,2,32,256]{3,2,1,0:T(8,128)S(1)} collective-permute-done((f32[4,2,32,256]{3,2,1,0:T(8,128)S(1)}, f32[4,2,32,256]{3,2,1,0:T(8,128)S(1)}, u32[]{:S(2)}, u32[]{:S(2)}) %collective-permute-start.13) | collective-permute-done | bytes 262176 | tf_op jit(solution)/shard_map/ppermute | solution.py:360
  47.7 0.6 merge0_0.1
  48.3 2.7 %collective-permute-start.14 = (f32[4,1,32,256]{3,2,1,0:T(8,128)S(1)}, f32[4,1,32,256]{3,2,1,0:T(8,128)S(1)}, u32[]{:S(2)}, u32[]{:S(2)}) collective-permute-start(f32[4,1,32,256]{3,2,1,0:T(8,128)S(1)} %get-tuple-element.58), channel_id=1, source_target_pairs={{0,16},{8,24},{16,0},{24,8},{1,17},{9,25},{17,1},{25,9},{2,18},{10... | collective-permute-start | bytes 393224 | tf_op jit(solution)/shard_map/ppermute | solution.py:360
  50.9 0.3 collective-permute-start.9
  51.2 4.3 %collective-permute-done.3.received = f32[4,2,32,256]{3,2,1,0:T(8,128)S(1)} collective-permute-done((f32[4,2,32,256]{3,2,1,0:T(8,128)S(1)}, f32[4,2,32,256]{3,2,1,0:T(8,128)S(1)}, u32[]{:S(2)}, u32[]{:S(2)}) %collective-permute-start.3) | collective-permute-done | bytes 262176 | tf_op jit(solution)/shard_map/ppermute | solution.py:360
  55.5 0.6 merge2_0.1
  56.1 0.6 collective-permute-start.4
  56.7 5.2 %collective-permute-done.14.received = f32[4,1,32,256]{3,2,1,0:T(8,128)S(1)} collective-permute-done((f32[4,1,32,256]{3,2,1,0:T(8,128)S(1)}, f32[4,1,32,256]{3,2,1,0:T(8,128)S(1)}, u32[]{:S(2)}, u32[]{:S(2)}) %collective-permute-start.14) | collective-permute-done | bytes 131104 | tf_op jit(solution)/shard_map/ppermute | solution.py:360
  62.0 1.2 %emit0.1.refs_0_ = f32[3,4,64,128]{3,2,1,0:T(8,128)} custom-call(s32[1,3]{1,0:T(1,128)S(1)} %bitcast.9, f32[4,1,32,256]{3,2,1,0:T(8,128)S(1)} %get-tuple-element.57.kept, f32[4,1,32,256]{3,2,1,0:T(8,128)S(1)} %collective-permute-done.14.received), custom_call_target="tpu_custom_call" | custom-call | tf_op jit(solution)/shard_map/emit0/pallas_call | solution.py:341
  63.2 1.5 %collective-permute-done.9.received = f32[4,1,32,256]{3,2,1,0:T(8,128)S(1)} collective-permute-done((f32[4,1,32,256]{3,2,1,0:T(8,128)S(1)}, f32[4,1,32,256]{3,2,1,0:T(8,128)S(1)}, u32[]{:S(2)}, u32[]{:S(2)}) %collective-permute-start.9) | collective-permute-done | bytes 131104 | tf_op jit(solution)/shard_map/ppermute | solution.py:360
  64.7 1.2 %emit1.1.refs_0_ = f32[3,4,64,128]{3,2,1,0:T(8,128)} custom-call(s32[1,3]{1,0:T(1,128)S(1)} %bitcast.10, f32[4,1,32,256]{3,2,1,0:T(8,128)S(1)} %get-tuple-element.48.kept, f32[4,1,32,256]{3,2,1,0:T(8,128)S(1)} %collective-permute-done.9.received, f32[3,4,64,128]{3,2,1,0:T(8,128)} %emit0.1.refs_0_), custom_call_target="tpu_custom_call", output_to_operand_aliasing={{}: (3, {})} | custom-call | tf_op jit(solution)/shard_map/emit1/pallas_call | solution.py:341
  66.0 0.2 collective-permute-done.4.received
  66.2 1.2 %emit2.1 = f32[3,4,64,128]{3,2,1,0:T(8,128)} custom-call(s32[1,3]{1,0:T(1,128)S(1)} %bitcast.11, f32[4,1,32,256]{3,2,1,0:T(8,128)S(1)} %get-tuple-element.39.kept, f32[4,1,32,256]{3,2,1,0:T(8,128)S(1)} %collective-permute-done.4.received, f32[3,4,64,128]{3,2,1,0:T(8,128)} %emit1.1.refs_0_), custom_call_target="tpu_custom_call", output_to_operand_aliasing={{}: (3, {})} | custom-call | tf_op jit(solution)/shard_map/emit2/pallas_call | solution.py:341
  (5 shorter events, 0.1 us)
Async XLA Ops:
  0.0 7.4 %copy-start.1 = (s32[3,1]{0,1:T(1,128)S(1)}, s32[3,1]{0,1:T(1,128)}, u32[]{:S(2)}) copy-start(s32[3,1]{0,1:T(1,128)} %param.7) | copy-start | bytes 40
  0.0 7.4 %copy-start.3 = (s32[3,2,1,1,2]{0,4,3,2,1:T(2,128)S(1)}, s32[3,2,1,1,2]{0,4,3,2,1:T(2,128)}, u32[]{:S(2)}) copy-start(s32[3,2,1,1,2]{0,4,3,2,1:T(2,128)} %param.6) | copy-start | bytes 148
  0.0 0.7 %copy-start = (s32[3,1]{0,1:T(1,128)S(1)}, s32[3,1]{0,1:T(1,128)}, u32[]{:S(2)}) copy-start(s32[3,1]{0,1:T(1,128)} %param.7) | copy-start | bytes 40
  0.7 0.7 %copy-start.2 = (s32[3,2,1,1,2]{0,4,3,2,1:T(2,128)S(1)}, s32[3,2,1,1,2]{0,4,3,2,1:T(2,128)}, u32[]{:S(2)}) copy-start(s32[3,2,1,1,2]{0,4,3,2,1:T(2,128)} %param.6) | copy-start | bytes 148
  6.8 11.6 %collective-permute-start.10 = (f32[4,192,128]{2,1,0:T(8,128)S(1)}, f32[4,192,128]{2,1,0:T(8,128)S(1)}, u32[]{:S(2)}, u32[]{:S(2)}) collective-permute-start(f32[4,192,128]{2,1,0:T(8,128)S(1)} %get-tuple-element.51.rim), channel_id=1, source_target_pairs={{0,1},{1,0},{2,3},{3,2},{4,5},{5,4},{6,7},{7,6},{8,9},{9,8},{10,11... | collective-permute-start | bytes 1179656 | tf_op jit(solution)/shard_map/ppermute | solution.py:355
  12.6 9.6 %collective-permute-start.5 = (f32[4,160,128]{2,1,0:T(8,128)S(1)}, f32[4,160,128]{2,1,0:T(8,128)S(1)}, u32[]{:S(2)}, u32[]{:S(2)}) collective-permute-start(f32[4,160,128]{2,1,0:T(8,128)S(1)} %get-tuple-element.42.rim), channel_id=1, source_target_pairs={{0,1},{1,0},{2,3},{3,2},{4,5},{5,4},{6,7},{7,6},{8,9},{9,8},{10,11... | collective-permute-start | bytes 983048 | tf_op jit(solution)/shard_map/ppermute | solution.py:355
  17.9 7.4 %collective-permute-start = (f32[4,160,128]{2,1,0:T(8,128)S(1)}, f32[4,160,128]{2,1,0:T(8,128)S(1)}, u32[]{:S(2)}, u32[]{:S(2)}) collective-permute-start(f32[4,160,128]{2,1,0:T(8,128)S(1)} %get-tuple-element.33.rim), channel_id=1, source_target_pairs={{0,1},{1,0},{2,3},{3,2},{4,5},{5,4},{6,7},{7,6},{8,9},{9,8},{10,11... | collective-permute-start | bytes 983048 | tf_op jit(solution)/shard_map/ppermute | solution.py:355
  18.6 15.8 %collective-permute-start.11 = (f32[4,4,8,256]{3,2,1,0:T(8,128)S(1)}, f32[4,4,8,256]{3,2,1,0:T(8,128)S(1)}, u32[]{:S(2)}, u32[]{:S(2)}) collective-permute-start(f32[4,4,8,256]{3,2,1,0:T(8,128)S(1)} %get-tuple-element.53), channel_id=1, source_target_pairs={{0,2},{2,4},{4,6},{6,0},{1,3},{3,5},{5,7},{7,1},{8,10},{10,12},{12... | collective-permute-start | bytes 393224 | tf_op jit(solution)/shard_map/ppermute | solution.py:355
  21.2 13.2 %collective-permute-start.12 = (f32[4,4,8,256]{3,2,1,0:T(8,128)S(1)}, f32[4,4,8,256]{3,2,1,0:T(8,128)S(1)}, u32[]{:S(2)}, u32[]{:S(2)}) collective-permute-start(f32[4,4,8,256]{3,2,1,0:T(8,128)S(1)} %get-tuple-element.54), channel_id=1, source_target_pairs={{0,6},{2,0},{4,2},{6,4},{1,7},{3,1},{5,3},{7,5},{8,14},{10,8},{12,... | collective-permute-start | bytes 393224 | tf_op jit(solution)/shard_map/ppermute | solution.py:355
  22.4 8.3 %collective-permute-start.6 = (f32[4,2,8,256]{3,2,1,0:T(8,128)S(1)}, f32[4,2,8,256]{3,2,1,0:T(8,128)S(1)}, u32[]{:S(2)}, u32[]{:S(2)}) collective-permute-start(f32[4,2,8,256]{3,2,1,0:T(8,128)S(1)} %get-tuple-element.44), channel_id=1, source_target_pairs={{0,2},{2,4},{4,6},{6,0},{1,3},{3,5},{5,7},{7,1},{8,10},{10,12},{12... | collective-permute-start | bytes 196616 | tf_op jit(solution)/shard_map/ppermute | solution.py:355
  23.4 9.3 %collective-permute-start.7 = (f32[4,2,8,256]{3,2,1,0:T(8,128)S(1)}, f32[4,2,8,256]{3,2,1,0:T(8,128)S(1)}, u32[]{:S(2)}, u32[]{:S(2)}) collective-permute-start(f32[4,2,8,256]{3,2,1,0:T(8,128)S(1)} %get-tuple-element.45), channel_id=1, source_target_pairs={{0,6},{2,0},{4,2},{6,4},{1,7},{3,1},{5,3},{7,5},{8,14},{10,8},{12,... | collective-permute-start | bytes 196616 | tf_op jit(solution)/shard_map/ppermute | solution.py:355
  25.5 9.5 %collective-permute-start.1 = (f32[4,2,8,256]{3,2,1,0:T(8,128)S(1)}, f32[4,2,8,256]{3,2,1,0:T(8,128)S(1)}, u32[]{:S(2)}, u32[]{:S(2)}) collective-permute-start(f32[4,2,8,256]{3,2,1,0:T(8,128)S(1)} %get-tuple-element.35), channel_id=1, source_target_pairs={{0,2},{2,4},{4,6},{6,0},{1,3},{3,5},{5,7},{7,1},{8,10},{10,12},{12... | collective-permute-start | bytes 196616 | tf_op jit(solution)/shard_map/ppermute | solution.py:355
  30.7 4.3 %collective-permute-start.2 = (f32[4,2,8,256]{3,2,1,0:T(8,128)S(1)}, f32[4,2,8,256]{3,2,1,0:T(8,128)S(1)}, u32[]{:S(2)}, u32[]{:S(2)}) collective-permute-start(f32[4,2,8,256]{3,2,1,0:T(8,128)S(1)} %get-tuple-element.36), channel_id=1, source_target_pairs={{0,6},{2,0},{4,2},{6,4},{1,7},{3,1},{5,3},{7,5},{8,14},{10,8},{12,... | collective-permute-start | bytes 196616 | tf_op jit(solution)/shard_map/ppermute | solution.py:355
  32.8 9.2 %collective-permute-start.8 = (f32[4,2,32,256]{3,2,1,0:T(8,128)S(1)}, f32[4,2,32,256]{3,2,1,0:T(8,128)S(1)}, u32[]{:S(2)}, u32[]{:S(2)}) collective-permute-start(f32[4,2,32,256]{3,2,1,0:T(8,128)S(1)} %get-tuple-element.47), channel_id=1, source_target_pairs={{0,8},{8,0},{16,24},{24,16},{1,9},{9,1},{17,25},{25,17},{2,10},{10... | collective-permute-start | bytes 786440 | tf_op jit(solution)/shard_map/ppermute | solution.py:360
  34.5 13.2 %collective-permute-start.13 = (f32[4,2,32,256]{3,2,1,0:T(8,128)S(1)}, f32[4,2,32,256]{3,2,1,0:T(8,128)S(1)}, u32[]{:S(2)}, u32[]{:S(2)}) collective-permute-start(f32[4,2,32,256]{3,2,1,0:T(8,128)S(1)} %get-tuple-element.56), channel_id=1, source_target_pairs={{0,8},{8,0},{16,24},{24,16},{1,9},{9,1},{17,25},{25,17},{2,10},{10... | collective-permute-start | bytes 786440 | tf_op jit(solution)/shard_map/ppermute | solution.py:360
  35.1 20.4 %collective-permute-start.3 = (f32[4,2,32,256]{3,2,1,0:T(8,128)S(1)}, f32[4,2,32,256]{3,2,1,0:T(8,128)S(1)}, u32[]{:S(2)}, u32[]{:S(2)}) collective-permute-start(f32[4,2,32,256]{3,2,1,0:T(8,128)S(1)} %get-tuple-element.38), channel_id=1, source_target_pairs={{0,8},{8,0},{16,24},{24,16},{1,9},{9,1},{17,25},{25,17},{2,10},{10... | collective-permute-start | bytes 786440 | tf_op jit(solution)/shard_map/ppermute | solution.py:360
  48.3 13.7 %collective-permute-start.14 = (f32[4,1,32,256]{3,2,1,0:T(8,128)S(1)}, f32[4,1,32,256]{3,2,1,0:T(8,128)S(1)}, u32[]{:S(2)}, u32[]{:S(2)}) collective-permute-start(f32[4,1,32,256]{3,2,1,0:T(8,128)S(1)} %get-tuple-element.58), channel_id=1, source_target_pairs={{0,16},{8,24},{16,0},{24,8},{1,17},{9,25},{17,1},{25,9},{2,18},{10... | collective-permute-start | bytes 393224 | tf_op jit(solution)/shard_map/ppermute | solution.py:360
  50.9 13.8 %collective-permute-start.9 = (f32[4,1,32,256]{3,2,1,0:T(8,128)S(1)}, f32[4,1,32,256]{3,2,1,0:T(8,128)S(1)}, u32[]{:S(2)}, u32[]{:S(2)}) collective-permute-start(f32[4,1,32,256]{3,2,1,0:T(8,128)S(1)} %get-tuple-element.49), channel_id=1, source_target_pairs={{0,16},{8,24},{16,0},{24,8},{1,17},{9,25},{17,1},{25,9},{2,18},{10... | collective-permute-start | bytes 393224 | tf_op jit(solution)/shard_map/ppermute | solution.py:360
  56.1 10.0 %collective-permute-start.4 = (f32[4,1,32,256]{3,2,1,0:T(8,128)S(1)}, f32[4,1,32,256]{3,2,1,0:T(8,128)S(1)}, u32[]{:S(2)}, u32[]{:S(2)}) collective-permute-start(f32[4,1,32,256]{3,2,1,0:T(8,128)S(1)} %get-tuple-element.40), channel_id=1, source_target_pairs={{0,16},{8,24},{16,0},{24,8},{1,17},{9,25},{17,1},{25,9},{2,18},{10... | collective-permute-start | bytes 393224 | tf_op jit(solution)/shard_map/ppermute | solution.py:360

commit v3 on v2

--- a/solution.py
+++ b/solution.py
@@ -7,6 +7,7 @@
 from jax.experimental.pallas import tpu as pltpu
 from jax.sharding import PartitionSpec as P
 
+
 MARGIN = 16
 JIT = 8
 VIEWS = 3
@@ -42,12 +43,13 @@
     return length + (1 if shared_spill(view, slices, phases) else 2) * TILE * phases
 
 
-def render_kernel(view, phases, offs, order, dens, emis, home, rim, dbuf, ebuf, drow, dcol, hs, rs, sem):
+def render_kernel(view, phases, offs, order, dens, emis, home, rim, turn, dbuf, ebuf, drow, dcol, hs, rs, sem):
     slices, length, columns = dens.shape
     bricks = columns // length
     half = length // 2
     quota = length // phases
     back = order[0, view] == 1
+    turn[...] = jnp.full(turn.shape, order[0, view], jnp.int32)
 
     def slice_at(k):
         return jnp.where(back, slices - 1 - k, k)
@@ -160,9 +162,13 @@
     assert bricks == 2 and length == 128
     return pl.pallas_call(
         functools.partial(render_kernel, view, phases),
-        out_shape=(near((4, rows, columns)), near((4, rows, length))),
+        out_shape=(
+            near((4, rows, columns)),
+            near((4, rows, length)),
+            pltpu.VMEM((TILE, 128), jnp.int32),
+        ),
         in_specs=[SMEM, SMEM, ANY, ANY],
-        out_specs=(VMEM, VMEM),
+        out_specs=(VMEM,) * 3,
         scratch_shapes=[
             pltpu.VMEM(density.shape, BF),
             pltpu.VMEM(emission.shape, BF),
@@ -173,8 +179,7 @@
             pltpu.SemaphoreType.DMA((2, slices)),
         ],
         compiler_params=pltpu.CompilerParams(vmem_limit_bytes=16 << 20),
-        name=f"render{view}",
-    )(offsets, orders, *(pltpu.with_memory_space_constraint(array, pltpu.HBM) for array in (density, emission)))
+    )(offsets, orders, density, emission)
 
 
 def joined(channel, one, other):
@@ -239,35 +244,38 @@
         in_specs=[VMEM] * 4,
         out_specs=(VMEM,) * 3,
         compiler_params=pltpu.CompilerParams(vmem_limit_bytes=4 << 20),
-        name=f"fold{view}",
     )(*held(home, rim, low, high))
 
 
+def spills(shared, c, p, pack, odd, above, below):
+    if not shared:
+        return above[c, p], below[c, p]
+    neutral = 1.0 if c == 3 else 0.0
+    sub = lax.broadcasted_iota(jnp.int32, above.shape[2:], 0)
+    top, bottom = above[c, pack], below[c, pack]
+    top = jnp.where(odd == 1, pltpu.roll(top, TILE // 2, 0), top)
+    bottom = jnp.where(odd == 1, pltpu.roll(bottom, TILE // 2, 0), bottom)
+    return (
+        jnp.where(sub < TILE // 2, top, neutral),
+        jnp.where(sub < TILE // 2, neutral, bottom),
+    )
+
+
 def finish_kernel(shared, canvas, above, below, kept, given):
-    me = lax.axis_index("depth")
-    bit = me & 1
+    bit = lax.axis_index("depth") & 1
     quota = canvas.shape[2]
     for n in range(kept.shape[1]):
         for out, odd in ((kept, bit), (given, 1 - bit)):
             p = 2 * n + odd
             for c in range(4):
-                if shared:
-                    neutral = 1.0 if c == 3 else 0.0
-                    sub = lax.broadcasted_iota(jnp.int32, above.shape[2:], 0)
-                    top, bottom = above[c, n], below[c, n]
-                    top = jnp.where(odd == 1, pltpu.roll(top, TILE // 2, 0), top)
-                    bottom = jnp.where(odd == 1, pltpu.roll(bottom, TILE // 2, 0), bottom)
-                    top = jnp.where(sub < TILE // 2, top, neutral)
-                    bottom = jnp.where(sub < TILE // 2, neutral, bottom)
-                else:
-                    top, bottom = above[c, p], below[c, p]
+                top, bottom = spills(shared, c, p, n, odd, above, below)
                 out[c, n, 0:TILE] = joined(c, canvas[c, p, 0:TILE], top)
                 if quota > 2 * TILE:
                     out[c, n, TILE : quota - TILE] = canvas[c, p, TILE : quota - TILE]
                 out[c, n, quota - TILE :] = joined(c, canvas[c, p, quota - TILE :], bottom)
 
 
-def finish(view, shared, canvas, above, below):
+def finish(shared, canvas, above, below):
     channels, phases, quota, columns = canvas.shape
     return pl.pallas_call(
         functools.partial(finish_kernel, shared),
@@ -275,79 +283,131 @@
         in_specs=[VMEM] * 3,
         out_specs=(VMEM,) * 2,
         compiler_params=pltpu.CompilerParams(vmem_limit_bytes=4 << 20),
-        name=f"finish{view}",
     )(*held(canvas, above, below))
 
 
-def over(own_first, own, other):
-    front = [jnp.where(own_first, a, b) for a, b in zip(own, other)]
-    rear = [jnp.where(own_first, b, a) for a, b in zip(own, other)]
+def over(ahead, own, other):
+    front = [jnp.where(ahead, a, b) for a, b in zip(own, other)]
+    rear = [jnp.where(ahead, b, a) for a, b in zip(own, other)]
     return [f + front[3] * r for f, r in zip(front[:3], rear[:3])] + [front[3] * rear[3]]
 
 
-def own_first(view, level, order):
+def own_ahead(level, turn, rows):
     me = lax.axis_index("depth")
-    return jnp.logical_xor((me >> level & 1) == 0, order[0, view] == 1)
-
-
-def merge_kernel(view, level, order, kept, received, next_kept, next_given):
-    ahead = own_first(view, level, order)
+    return jnp.broadcast_to(turn[0:1, :], (rows, turn.shape[1])) == (me >> level & 1)
+
+
+def chunks(columns, lanes):
+    return [slice(n, n + lanes) for n in range(0, columns, lanes)]
+
+
+def merge_kernel(level, turn, kept, received, next_kept, next_given):
+    quota, columns = kept.shape[2:]
+    ahead = own_ahead(level, turn, quota)
     bit = lax.axis_index("depth") >> (level + 1) & 1
     for n in range(next_kept.shape[1]):
         for out, odd in ((next_kept, bit), (next_given, 1 - bit)):
             p = 2 * n + odd
-            pixels = over(ahead, [kept[c, p] for c in range(4)], [received[c, p] for c in range(4)])
+            for part in chunks(columns, turn.shape[1]):
+                own = [kept[c, p, :, part] for c in range(4)]
+                other = [received[c, p, :, part] for c in range(4)]
+                for c, pixels in enumerate(over(ahead, own, other)):
+                    out[c, n, :, part] = pixels
+
+
+def merge(level, turn, kept, received):
+    channels, phases, quota, columns = kept.shape
+    return pl.pallas_call(
+        functools.partial(merge_kernel, level),
+        out_shape=(near((channels, phases // 2, quota, columns)),) * 2,
+        in_specs=[VMEM] * 3,
+        out_specs=(VMEM,) * 2,
+        compiler_params=pltpu.CompilerParams(vmem_limit_bytes=4 << 20),
+    )(*held(turn, kept, received))
+
+
+def emit_kernel(view, level, groups, turn, *refs):
+    out, stage, sem = refs[-3:]
+    lanes = stage.shape[2]
+    start = 0
+    for (indices, at, size) in groups:
+        for n, part in enumerate(chunks(refs[indices[0]].shape[-1], lanes)):
+            layers = [[refs[i][c, at : at + size, part] for c in range(4)] for i in indices]
+            bit = level
+            while len(layers) > 1:
+                ahead = own_ahead(bit, turn, size)
+                layers = [over(ahead, one, other) for one, other in zip(layers[0::2], layers[1::2])]
+                bit += 1
+            pieces = refs[indices[0]].shape[-1] // lanes
             for c in range(4):
-                out[c, n] = pixels[c]
-
-
-def merge(view, level, orders, kept, received):
-    channels, phases, quota, columns = kept.shape
-    return pl.pallas_call(
-        functools.partial(merge_kernel, view, level),
-        out_shape=(near((channels, phases // 2, quota, columns)),) * 2,
-        in_specs=[SMEM] + [VMEM] * 2,
-        out_specs=(VMEM,) * 2,
-        compiler_params=pltpu.CompilerParams(vmem_limit_bytes=4 << 20),
-        name=f"merge{view}_{level}",
-    )(orders, *held(kept, received))
-
-
-def emit_kernel(view, level, order, kept, received, *refs):
-    out, stage, sem = refs[-3:]
-    ahead = own_first(view, level, order)
-    quota, columns = kept.shape[2:]
-    lanes = stage.shape[2]
-    pieces = columns // lanes
-    pixels = over(ahead, [kept[c, 0] for c in range(4)], [received[c, 0] for c in range(4)])
-    for c in range(4):
-        for n in range(pieces):
-            stage[c, pl.ds(n, quota, stride=pieces), :] = pixels[c][:, n * lanes : (n + 1) * lanes]
+                stage[c, pl.ds(start * pieces + n, size, stride=pieces), :] = layers[0][c]
+        start += size
     copy = pltpu.make_async_copy(stage, out.at[view], sem)
     copy.start()
     copy.wait()
 
 
-def emit(view, level, orders, kept, received, image):
-    channels, _, quota, columns = kept.shape
+def emit(view, level, turn, blocks, groups, image):
+    channels, _, columns = blocks[0].shape
+    quota = sum(size for _, _, size in groups)
     shape = (channels, quota * columns // 128, 128)
-    operands = [orders, *held(kept, received)]
-    specs = [SMEM, VMEM, VMEM]
+    operands = held(turn, *blocks)
+    specs = [VMEM] * len(operands)
     aliases = {}
     if image is not None:
+        aliases = {len(operands): 0}
         operands.append(image)
         specs.append(ANY)
-        aliases = {3: 0}
-    return pl.pallas_call(
-        functools.partial(emit_kernel, view, level),
+    return pl.pallas_call(
+        functools.partial(emit_kernel, view, level, groups),
         out_shape=jax.ShapeDtypeStruct((VIEWS,) + shape, F32),
         in_specs=specs,
         out_specs=ANY,
         scratch_shapes=[pltpu.VMEM(shape, F32), pltpu.SemaphoreType.DMA],
         input_output_aliases=aliases,
         compiler_params=pltpu.CompilerParams(vmem_limit_bytes=4 << 20),
-        name=f"emit{view}",
     )(*operands)
+
+
+def inner_kernel(canvas, *outs):
+    me = lax.axis_index("depth")
+    for k, out in enumerate(outs):
+        out[...] = canvas[:, me ^ k, TILE : TILE + out.shape[1]]
+
+
+def split_inner(canvas):
+    channels, phases, quota, columns = canvas.shape
+    if quota == 2 * TILE:
+        return []
+    return pl.pallas_call(
+        inner_kernel,
+        out_shape=(near((channels, quota - 2 * TILE, columns)),) * phases,
+        in_specs=[VMEM],
+        out_specs=(VMEM,) * phases,
+        compiler_params=pltpu.CompilerParams(vmem_limit_bytes=4 << 20),
+    )(*held(canvas))
+
+
+def edge_kernel(shared, canvas, above, below, *outs):
+    me = lax.axis_index("depth")
+    quota = canvas.shape[2]
+    for k, out in enumerate(outs):
+        p = me ^ k
+        for c in range(4):
+            top, bottom = spills(shared, c, p, p >> 1, p & 1, above, below)
+            out[c, 0:TILE] = joined(c, canvas[c, p, 0:TILE], top)
+            out[c, TILE:] = joined(c, canvas[c, p, quota - TILE :], bottom)
+
+
+def split_edges(shared, canvas, above, below):
+    channels, phases, _, columns = canvas.shape
+    return pl.pallas_call(
+        functools.partial(edge_kernel, shared),
+        out_shape=(near((channels, 2 * TILE, columns)),) * phases,
+        in_specs=[VMEM] * 3,
+        out_specs=(VMEM,) * phases,
+        compiler_params=pltpu.CompilerParams(vmem_limit_bytes=4 << 20),
+    )(*held(canvas, above, below))
 
 
 def shifted(block, axis, step):
@@ -355,31 +415,59 @@
     return lax.ppermute(block, axis, [(i, (i + step) % count) for i in range(count)])
 
 
-def swapped(block, level):
+def swapped(block, flip):
     count = lax.axis_size("depth")
-    return lax.ppermute(block, "depth", [(i, i ^ 1 << level) for i in range(count)])
+    return lax.ppermute(block, "depth", [(i, i ^ flip) for i in range(count)])
+
+
+def canvas_of(view, density, emission, offsets, orders):
+    slices, length = density.shape[:2]
+    phases = lax.axis_size("depth")
+    home, rim, turn = render(view, phases, offsets, orders, density, emission)
+    low = shifted(rim, "col", 1)
+    high = low if lax.axis_size("col") == 2 else shifted(rim, "col", -1)
+    canvas, up, down = fold(view, slices, length, phases, home, rim, low, high)
+    above = shifted(down, "row", 1)
+    below = shifted(up, "row", -1)
+    return canvas, above, below, turn
 
 
 def local(density, emission, offsets, view_order):
     slices, length, columns = density.shape
     phases = lax.axis_size("depth")
     levels = phases.bit_length() - 1
+    quota = length // phases
     offsets = offsets.transpose(1, 2, 3, 4, 0)
     orders = view_order.transpose(1, 0)
+    density, emission, offsets, orders = (
+        pltpu.with_memory_space_constraint(array, pltpu.HBM)
+        for array in (density, emission, offsets, orders)
+    )
     image = None
     for view in range(VIEWS):
         shared = shared_spill(view, slices, phases)
-        home, rim = render(view, phases, offsets, orders, density, emission)
-        low = shifted(rim, "col", 1)
-        high = low if lax.axis_size("col") == 2 else shifted(rim, "col", -1)
-        canvas, up, down = fold(view, slices, length, phases, home, rim, low, high)
-        above = shifted(down, "row", 1)
-        below = shifted(up, "row", -1)
-        kept, given = finish(view, shared, canvas, above, below)
-        for level in range(levels - 1):
-            kept, given = merge(view, level, orders, kept, swapped(given, level))
-        image = emit(view, levels - 1, orders, kept, swapped(given, levels - 1), image)
-    return image.reshape(VIEWS, 4, length // phases, 1, columns)
+        canvas, above, below, turn = canvas_of(view, density, emission, offsets, orders)
+        if view < VIEWS - 1:
+            kept, given = finish(shared, canvas, above, below)
+            for level in range(levels - 1):
+                received = swapped(given, 1 << level)
+                kept, given = merge(level, turn, kept, received)
+            received = swapped(given, 1 << levels - 1)
+            blocks = [kept[:, 0], received[:, 0]]
+            groups = (((0, 1), 0, quota),)
+            image = emit(view, levels - 1, turn, blocks, groups, image)
+        else:
+            inner = split_inner(canvas)
+            inner = [swapped(b, k) if k else b for k, b in enumerate(inner)]
+            edges = split_edges(shared, canvas, above, below)
+            edges = [swapped(b, k) if k else b for k, b in enumerate(edges)]
+            which = tuple(range(phases))
+            groups = ((which, 0, TILE),)
+            if inner:
+                groups += ((tuple(phases + k for k in which), 0, quota - 2 * TILE),)
+            groups += ((which, TILE, TILE),)
+            image = emit(view, 0, turn, [*edges, *inner], groups, image)
+    return image.reshape(VIEWS, 4, quota, 1, columns)
 
 
 def solution(mesh):

time: 67.6 us -> 62.3 us (0.922)
  waiting for transfers between devices: 25.8 us -> 14.8 us
  starting transfers between devices: 18.1 us -> 28 us
  Pallas kernels: 22 us -> 19.1 us
  local copies, waits for them, and re-layouts: 1.41 us -> 0 us
    ppermute x6 -> x10, starting transfers between devices: 7.84 us -> 17.3 us  [swapped(): return lax.ppermute(block, 'depth', [(i, i ^ flip) for i in range(count)])]
    ppermute x6 -> x10, waiting for transfers between devices: 21.1 us -> 13.8 us  [swapped(): return lax.ppermute(block, 'depth', [(i, i ^ flip) for i in range(count)])]
    ppermute x9, waiting for transfers between devices: 4.67 us -> 0.94 us  [shifted(): lax.ppermute(block, axis, [(i, (i + step) % count) for i in range(count)])]
    pallas_call x6 -> x7, Pallas kernels: 5.5 us -> 2.27 us  [the longest x3 2.11 us: emit(): pl.pallas_call(functools.partial(emit_kernel, view, level, groups), out_s...]
    unnamed x8 -> x0, local copies, waits for them, and re-layouts: 1.41 us -> none
  transfers between devices with their start and end apart: 15 -> 19, of which waited for: 7 -> 4; matrix products, arithmetic and copies ran while one was open for 0% -> 0% of each run, Pallas kernels for 23% -> 21%
where the time goes in v3:
time: 62.3 us; the launch traced here: 62 us
  starting transfers between devices  28 us (45%)
  Pallas kernels  19.1 us (31%)
  waiting for transfers between devices  14.8 us (24%)
    ppermute x10, starting transfers between devices, swapped(): return lax.ppermute(block, 'depth', [(i, i ^ flip) for i in range(count)])  17.3 us
    pallas_call x3, Pallas kernels, render(): pl.pallas_call(functools.partial(render_kernel, view, phases), out_shape=...  16.2 us
    ppermute x10, waiting for transfers between devices, swapped(): return lax.ppermute(block, 'depth', [(i, i ^ flip) for i in range(count)])  13.8 us
    ppermute x9, starting transfers between devices, shifted(): lax.ppermute(block, axis, [(i, (i + step) % count) for i in range(count)])  10.7 us
    pallas_call x3, Pallas kernels, emit(): pl.pallas_call(functools.partial(emit_kernel, view, level, groups), out_s...  2.11 us
  transfers between devices with their start and end apart: 19, of which 4 were waited for; matrix products, arithmetic and copies ran while one was open for 0% of the time, Pallas kernels for 21%

profile of v3, /device:TPU:0, one launch (start us, length us, event | category | flops | bytes accessed | tf_op | source)
XLA Modules:
  0.0 62.0 jit_solution(10783303846398466258)
XLA Ops:
  0.0 5.6 %shard_map.54 = (f32[4,192,256]{2,1,0:T(8,128)S(1)}, f32[4,192,128]{2,1,0:T(8,128)S(1)}, s32[8,128]{1,0:T(8,128)S(1)}) custom-call(s32[2,1,1,2,3]{4,3,2,1,0:T(2,128)} %bitcast.15, s32[1,3]{1,0:T(1,128)} %bitcast.18, bf16[8,128,256]{2,1,0:T(8,128)(2,1)} %dens.5, bf16[3,8,128,256]{3,2,1,0:T(8,128)(2,1)} %emis.5), custom_call_target="tpu_custom_call" | custom-call | tf_op jit(solution)/shard_map/pallas_call | solution.py:163
  5.6 0.6 collective-permute-start.14
  6.1 5.3 %shard_map.50 = (f32[4,160,256]{2,1,0:T(8,128)S(1)}, f32[4,160,128]{2,1,0:T(8,128)S(1)}, s32[8,128]{1,0:T(8,128)S(1)}) custom-call(s32[2,1,1,2,3]{4,3,2,1,0:T(2,128)} %bitcast.16, s32[1,3]{1,0:T(1,128)} %bitcast.19, bf16[8,128,256]{2,1,0:T(8,128)(2,1)} %dens.5, bf16[3,8,128,256]{3,2,1,0:T(8,128)(2,1)} %emis.5), custom_call_target="tpu_custom_call" | custom-call | tf_op jit(solution)/shard_map/pallas_call | solution.py:163
  11.5 0.1 collective-permute-start.9
  11.6 0.0 collective-permute-done.14.low.high
  11.6 0.2 shard_map.55
  11.7 3.0 %collective-permute-start.15 = (f32[4,4,8,256]{3,2,1,0:T(8,128)S(1)}, f32[4,4,8,256]{3,2,1,0:T(8,128)S(1)}, u32[]{:S(2)}, u32[]{:S(2)}) collective-permute-start(f32[4,4,8,256]{3,2,1,0:T(8,128)S(1)} %get-tuple-element.67), channel_id=1, source_target_pairs={{0,2},{2,4},{4,6},{6,0},{1,3},{3,5},{5,7},{7,1},{8,10},{10,12},{12... | collective-permute-start | bytes 393224 | tf_op jit(solution)/shard_map/ppermute | solution.py:415
  14.7 1.0 %collective-permute-start.16 = (f32[4,4,8,256]{3,2,1,0:T(8,128)S(1)}, f32[4,4,8,256]{3,2,1,0:T(8,128)S(1)}, u32[]{:S(2)}, u32[]{:S(2)}) collective-permute-start(f32[4,4,8,256]{3,2,1,0:T(8,128)S(1)} %get-tuple-element.68), channel_id=1, source_target_pairs={{0,6},{2,0},{4,2},{6,4},{1,7},{3,1},{5,3},{7,5},{8,14},{10,8},{12,... | collective-permute-start | bytes 393224 | tf_op jit(solution)/shard_map/ppermute | solution.py:415
  15.8 0.0 collective-permute-done.9.low.high
  15.8 0.2 shard_map.51
  15.9 1.0 %collective-permute-start.10 = (f32[4,2,8,256]{3,2,1,0:T(8,128)S(1)}, f32[4,2,8,256]{3,2,1,0:T(8,128)S(1)}, u32[]{:S(2)}, u32[]{:S(2)}) collective-permute-start(f32[4,2,8,256]{3,2,1,0:T(8,128)S(1)} %get-tuple-element.57), channel_id=1, source_target_pairs={{0,2},{2,4},{4,6},{6,0},{1,3},{3,5},{5,7},{7,1},{8,10},{10,12},{12... | collective-permute-start | bytes 196616 | tf_op jit(solution)/shard_map/ppermute | solution.py:415
  17.0 1.9 %collective-permute-start.11 = (f32[4,2,8,256]{3,2,1,0:T(8,128)S(1)}, f32[4,2,8,256]{3,2,1,0:T(8,128)S(1)}, u32[]{:S(2)}, u32[]{:S(2)}) collective-permute-start(f32[4,2,8,256]{3,2,1,0:T(8,128)S(1)} %get-tuple-element.58), channel_id=1, source_target_pairs={{0,6},{2,0},{4,2},{6,4},{1,7},{3,1},{5,3},{7,5},{8,14},{10,8},{12,... | collective-permute-start | bytes 196616 | tf_op jit(solution)/shard_map/ppermute | solution.py:415
  18.9 5.3 %shard_map.46 = (f32[4,160,256]{2,1,0:T(8,128)S(1)}, f32[4,160,128]{2,1,0:T(8,128)S(1)}, s32[8,128]{1,0:T(8,128)S(1)}) custom-call(s32[2,1,1,2,3]{4,3,2,1,0:T(2,128)} %bitcast.17, s32[1,3]{1,0:T(1,128)} %bitcast.20, bf16[8,128,256]{2,1,0:T(8,128)(2,1)} %dens.5, bf16[3,8,128,256]{3,2,1,0:T(8,128)(2,1)} %emis.5), custom_call_target="tpu_custom_call" | custom-call | tf_op jit(solution)/shard_map/pallas_call | solution.py:163
  24.2 0.1 collective-permute-start
  24.3 0.0 collective-permute-done.10.above
  24.3 0.9 %collective-permute-done.11.below = f32[4,2,8,256]{3,2,1,0:T(8,128)S(1)} collective-permute-done((f32[4,2,8,256]{3,2,1,0:T(8,128)S(1)}, f32[4,2,8,256]{3,2,1,0:T(8,128)S(1)}, u32[]{:S(2)}, u32[]{:S(2)}) %collective-permute-start.11) | collective-permute-done | bytes 65568 | tf_op jit(solution)/shard_map/ppermute | solution.py:415
  25.3 1.6 %collective-permute-start.12 = (f32[4,2,32,256]{3,2,1,0:T(8,128)S(1)}, f32[4,2,32,256]{3,2,1,0:T(8,128)S(1)}, u32[]{:S(2)}, u32[]{:S(2)}) collective-permute-start(f32[4,2,32,256]{3,2,1,0:T(8,128)S(1)} %get-tuple-element.60), channel_id=1, source_target_pairs={{0,8},{8,0},{16,24},{24,16},{1,9},{9,1},{17,25},{25,17},{2,10},{10... | collective-permute-start | bytes 786440 | tf_op jit(solution)/shard_map/ppermute | solution.py:420
  27.0 0.0 collective-permute-done.15.above
  27.0 0.0 collective-permute-done.16.below
  27.0 0.1 shard_map.56
  27.0 0.5 collective-permute-start.17
  27.5 7.0 %collective-permute-done.12.received = f32[4,2,32,256]{3,2,1,0:T(8,128)S(1)} collective-permute-done((f32[4,2,32,256]{3,2,1,0:T(8,128)S(1)}, f32[4,2,32,256]{3,2,1,0:T(8,128)S(1)}, u32[]{:S(2)}, u32[]{:S(2)}) %collective-permute-start.12) | collective-permute-done | bytes 262176 | tf_op jit(solution)/shard_map/ppermute | solution.py:420
  34.6 2.7 %collective-permute-start.13 = (f32[4,1,32,256]{3,2,0,1:T(8,128)S(1)}, f32[4,1,32,256]{3,2,0,1:T(8,128)S(1)}, u32[]{:S(2)}, u32[]{:S(2)}) collective-permute-start(f32[4,1,32,256]{3,2,0,1:T(8,128)S(1)} %bitcast.13), channel_id=1, source_target_pairs={{0,16},{8,24},{16,0},{24,8},{1,17},{9,25},{17,1},{25,9},{2,18},{10... | collective-permute-start | bytes 393224 | tf_op jit(solution)/shard_map/ppermute | solution.py:420
  37.3 4.6 %collective-permute-done.17.received = f32[4,2,32,256]{3,2,1,0:T(8,128)S(1)} collective-permute-done((f32[4,2,32,256]{3,2,1,0:T(8,128)S(1)}, f32[4,2,32,256]{3,2,1,0:T(8,128)S(1)}, u32[]{:S(2)}, u32[]{:S(2)}) %collective-permute-start.17) | collective-permute-done | bytes 262176 | tf_op jit(solution)/shard_map/ppermute | solution.py:420
  41.9 1.0 %collective-permute-start.18 = (f32[4,1,32,256]{3,2,0,1:T(8,128)S(1)}, f32[4,1,32,256]{3,2,0,1:T(8,128)S(1)}, u32[]{:S(2)}, u32[]{:S(2)}) collective-permute-start(f32[4,1,32,256]{3,2,0,1:T(8,128)S(1)} %bitcast.14), channel_id=1, source_target_pairs={{0,16},{8,24},{16,0},{24,8},{1,17},{9,25},{17,1},{25,9},{2,18},{10... | collective-permute-start | bytes 393224 | tf_op jit(solution)/shard_map/ppermute | solution.py:420
  42.9 0.0 collective-permute-done.low.high
  42.9 0.2 shard_map.47
  43.1 0.8 %collective-permute-start.1 = (f32[4,2,8,256]{3,2,1,0:T(8,128)S(1)}, f32[4,2,8,256]{3,2,1,0:T(8,128)S(1)}, u32[]{:S(2)}, u32[]{:S(2)}) collective-permute-start(f32[4,2,8,256]{3,2,1,0:T(8,128)S(1)} %get-tuple-element.43), channel_id=1, source_target_pairs={{0,2},{2,4},{4,6},{6,0},{1,3},{3,5},{5,7},{7,1},{8,10},{10,12},{12... | collective-permute-start | bytes 196616 | tf_op jit(solution)/shard_map/ppermute | solution.py:415
  43.9 2.1 %collective-permute-start.2 = (f32[4,2,8,256]{3,2,1,0:T(8,128)S(1)}, f32[4,2,8,256]{3,2,1,0:T(8,128)S(1)}, u32[]{:S(2)}, u32[]{:S(2)}) collective-permute-start(f32[4,2,8,256]{3,2,1,0:T(8,128)S(1)} %get-tuple-element.44), channel_id=1, source_target_pairs={{0,6},{2,0},{4,2},{6,4},{1,7},{3,1},{5,3},{7,5},{8,14},{10,8},{12,... | collective-permute-start | bytes 196616 | tf_op jit(solution)/shard_map/ppermute | solution.py:415
  46.1 2.5 %collective-permute-start.6 = (f32[4,16,256]{2,1,0:T(8,128)S(1)}, f32[4,16,256]{2,1,0:T(8,128)S(1)}, u32[]{:S(2)}, u32[]{:S(2)}) collective-permute-start(f32[4,16,256]{2,1,0:T(8,128)S(1)} %get-tuple-element.50), channel_id=1, source_target_pairs={{0,8},{8,0},{16,24},{24,16},{1,9},{9,1},{17,25},{25,17},{2,10},{10... | collective-permute-start | bytes 196616 | tf_op jit(solution)/shard_map/ppermute | solution.py:420
  48.6 0.0 collective-permute-done.1.above
  48.6 1.6 %collective-permute-start.7 = (f32[4,16,256]{2,1,0:T(8,128)S(1)}, f32[4,16,256]{2,1,0:T(8,128)S(1)}, u32[]{:S(2)}, u32[]{:S(2)}) collective-permute-start(f32[4,16,256]{2,1,0:T(8,128)S(1)} %get-tuple-element.51), channel_id=1, source_target_pairs={{0,16},{8,24},{16,0},{24,8},{1,17},{9,25},{17,1},{25,9},{2,18},{10... | collective-permute-start | bytes 196616 | tf_op jit(solution)/shard_map/ppermute | solution.py:420
  50.2 0.0 collective-permute-done.2.below
  50.2 2.9 %collective-permute-start.8 = (f32[4,16,256]{2,1,0:T(8,128)S(1)}, f32[4,16,256]{2,1,0:T(8,128)S(1)}, u32[]{:S(2)}, u32[]{:S(2)}) collective-permute-start(f32[4,16,256]{2,1,0:T(8,128)S(1)} %get-tuple-element.52), channel_id=1, source_target_pairs={{0,24},{8,16},{16,8},{24,0},{1,25},{9,17},{17,9},{25,1},{2,26},{10... | collective-permute-start | bytes 196616 | tf_op jit(solution)/shard_map/ppermute | solution.py:420
  53.1 0.1 shard_map.48
  53.2 0.0 collective-permute-done.6.refs_5_
  53.2 0.1 collective-permute-start.3
  53.3 0.0 collective-permute-done.13
  53.3 1.5 %collective-permute-start.4 = (f32[4,16,256]{2,1,0:T(8,128)S(1)}, f32[4,16,256]{2,1,0:T(8,128)S(1)}, u32[]{:S(2)}, u32[]{:S(2)}) collective-permute-start(f32[4,16,256]{2,1,0:T(8,128)S(1)} %get-tuple-element.47), channel_id=1, source_target_pairs={{0,16},{8,24},{16,0},{24,8},{1,17},{9,25},{17,1},{25,9},{2,18},{10... | collective-permute-start | bytes 196616 | tf_op jit(solution)/shard_map/ppermute | solution.py:420
  54.8 0.0 collective-permute-done.18
  54.8 2.9 %collective-permute-start.5 = (f32[4,16,256]{2,1,0:T(8,128)S(1)}, f32[4,16,256]{2,1,0:T(8,128)S(1)}, u32[]{:S(2)}, u32[]{:S(2)}) collective-permute-start(f32[4,16,256]{2,1,0:T(8,128)S(1)} %get-tuple-element.48), channel_id=1, source_target_pairs={{0,24},{8,16},{16,8},{24,0},{1,25},{9,17},{17,9},{25,1},{2,26},{10... | collective-permute-start | bytes 196616 | tf_op jit(solution)/shard_map/ppermute | solution.py:420
  57.6 0.7 %shard_map.58.refs_2_ = f32[3,4,64,128]{3,2,1,0:T(8,128)} custom-call(s32[8,128]{1,0:T(8,128)S(1)} %get-tuple-element.63.turn, f32[4,32,256]{2,1,0:T(8,128)S(1)} %bitcast.9, f32[4,32,256]{2,1,0:T(8,128)S(1)} %bitcast.10), custom_call_target="tpu_custom_call" | custom-call | tf_op jit(solution)/shard_map/pallas_call | solution.py:361
  58.3 0.7 %shard_map.59.refs_8_ = f32[3,4,64,128]{3,2,1,0:T(8,128)} custom-call(s32[8,128]{1,0:T(8,128)S(1)} %get-tuple-element.53.turn, f32[4,32,256]{2,1,0:T(8,128)S(1)} %bitcast.11, f32[4,32,256]{2,1,0:T(8,128)S(1)} %bitcast.12, f32[3,4,64,128]{3,2,1,0:T(8,128)} %shard_map.58.refs_2_), custom_call_target="tpu_custom_call", output_to_operand_aliasing={{}: (3, {})} | custom-call | tf_op jit(solution)/shard_map/pallas_call | solution.py:361
  59.0 0.0 collective-permute-done.7.refs_6_
  59.1 0.0 collective-permute-done.3.refs_1_
  59.1 2.2 %collective-permute-done.4.refs_2_ = f32[4,16,256]{2,1,0:T(8,128)S(1)} collective-permute-done((f32[4,16,256]{2,1,0:T(8,128)S(1)}, f32[4,16,256]{2,1,0:T(8,128)S(1)}, u32[]{:S(2)}, u32[]{:S(2)}) %collective-permute-start.4) | collective-permute-done | bytes 65568 | tf_op jit(solution)/shard_map/ppermute | solution.py:420
  61.3 0.0 collective-permute-done.5.refs_3_
  61.3 0.7 %shard_map.60 = f32[3,4,64,128]{3,2,1,0:T(8,128)} custom-call(s32[8,128]{1,0:T(8,128)S(1)} %get-tuple-element.39.turn, f32[4,16,256]{2,1,0:T(8,128)S(1)} %get-tuple-element.45.refs_0_, f32[4,16,256]{2,1,0:T(8,128)S(1)} %collective-permute-done.3.refs_1_, f32[4,16,256]{2,1,0:T(8,128)S(1)} %collective-permute-done.4.refs_2_, ...), custom_call_target="tpu_custom_call", output_to_operand_aliasing={{}: (9, {})} | custom-call | tf_op jit(solution)/shard_map/pallas_call | solution.py:361
  (5 shorter events, 0.2 us)
Async XLA Ops:
  5.6 6.0 %collective-permute-start.14 = (f32[4,192,128]{2,1,0:T(8,128)S(1)}, f32[4,192,128]{2,1,0:T(8,128)S(1)}, u32[]{:S(2)}, u32[]{:S(2)}) collective-permute-start(f32[4,192,128]{2,1,0:T(8,128)S(1)} %get-tuple-element.65.rim), channel_id=1, source_target_pairs={{0,1},{1,0},{2,3},{3,2},{4,5},{5,4},{6,7},{7,6},{8,9},{9,8},{10,11... | collective-permute-start | bytes 1179656 | tf_op jit(solution)/shard_map/ppermute | solution.py:415
  11.5 4.3 %collective-permute-start.9 = (f32[4,160,128]{2,1,0:T(8,128)S(1)}, f32[4,160,128]{2,1,0:T(8,128)S(1)}, u32[]{:S(2)}, u32[]{:S(2)}) collective-permute-start(f32[4,160,128]{2,1,0:T(8,128)S(1)} %get-tuple-element.55.rim), channel_id=1, source_target_pairs={{0,1},{1,0},{2,3},{3,2},{4,5},{5,4},{6,7},{7,6},{8,9},{9,8},{10,11... | collective-permute-start | bytes 983048 | tf_op jit(solution)/shard_map/ppermute | solution.py:415
  11.7 15.2 %collective-permute-start.15 = (f32[4,4,8,256]{3,2,1,0:T(8,128)S(1)}, f32[4,4,8,256]{3,2,1,0:T(8,128)S(1)}, u32[]{:S(2)}, u32[]{:S(2)}) collective-permute-start(f32[4,4,8,256]{3,2,1,0:T(8,128)S(1)} %get-tuple-element.67), channel_id=1, source_target_pairs={{0,2},{2,4},{4,6},{6,0},{1,3},{3,5},{5,7},{7,1},{8,10},{10,12},{12... | collective-permute-start | bytes 393224 | tf_op jit(solution)/shard_map/ppermute | solution.py:415
  14.7 12.2 %collective-permute-start.16 = (f32[4,4,8,256]{3,2,1,0:T(8,128)S(1)}, f32[4,4,8,256]{3,2,1,0:T(8,128)S(1)}, u32[]{:S(2)}, u32[]{:S(2)}) collective-permute-start(f32[4,4,8,256]{3,2,1,0:T(8,128)S(1)} %get-tuple-element.68), channel_id=1, source_target_pairs={{0,6},{2,0},{4,2},{6,4},{1,7},{3,1},{5,3},{7,5},{8,14},{10,8},{12,... | collective-permute-start | bytes 393224 | tf_op jit(solution)/shard_map/ppermute | solution.py:415
  15.9 8.4 %collective-permute-start.10 = (f32[4,2,8,256]{3,2,1,0:T(8,128)S(1)}, f32[4,2,8,256]{3,2,1,0:T(8,128)S(1)}, u32[]{:S(2)}, u32[]{:S(2)}) collective-permute-start(f32[4,2,8,256]{3,2,1,0:T(8,128)S(1)} %get-tuple-element.57), channel_id=1, source_target_pairs={{0,2},{2,4},{4,6},{6,0},{1,3},{3,5},{5,7},{7,1},{8,10},{10,12},{12... | collective-permute-start | bytes 196616 | tf_op jit(solution)/shard_map/ppermute | solution.py:415
  17.0 8.3 %collective-permute-start.11 = (f32[4,2,8,256]{3,2,1,0:T(8,128)S(1)}, f32[4,2,8,256]{3,2,1,0:T(8,128)S(1)}, u32[]{:S(2)}, u32[]{:S(2)}) collective-permute-start(f32[4,2,8,256]{3,2,1,0:T(8,128)S(1)} %get-tuple-element.58), channel_id=1, source_target_pairs={{0,6},{2,0},{4,2},{6,4},{1,7},{3,1},{5,3},{7,5},{8,14},{10,8},{12,... | collective-permute-start | bytes 196616 | tf_op jit(solution)/shard_map/ppermute | solution.py:415
  24.2 18.6 %collective-permute-start = (f32[4,160,128]{2,1,0:T(8,128)S(1)}, f32[4,160,128]{2,1,0:T(8,128)S(1)}, u32[]{:S(2)}, u32[]{:S(2)}) collective-permute-start(f32[4,160,128]{2,1,0:T(8,128)S(1)} %get-tuple-element.41.rim), channel_id=1, source_target_pairs={{0,1},{1,0},{2,3},{3,2},{4,5},{5,4},{6,7},{7,6},{8,9},{9,8},{10,11... | collective-permute-start | bytes 983048 | tf_op jit(solution)/shard_map/ppermute | solution.py:415
  25.3 9.2 %collective-permute-start.12 = (f32[4,2,32,256]{3,2,1,0:T(8,128)S(1)}, f32[4,2,32,256]{3,2,1,0:T(8,128)S(1)}, u32[]{:S(2)}, u32[]{:S(2)}) collective-permute-start(f32[4,2,32,256]{3,2,1,0:T(8,128)S(1)} %get-tuple-element.60), channel_id=1, source_target_pairs={{0,8},{8,0},{16,24},{24,16},{1,9},{9,1},{17,25},{25,17},{2,10},{10... | collective-permute-start | bytes 786440 | tf_op jit(solution)/shard_map/ppermute | solution.py:420
  27.0 14.8 %collective-permute-start.17 = (f32[4,2,32,256]{3,2,1,0:T(8,128)S(1)}, f32[4,2,32,256]{3,2,1,0:T(8,128)S(1)}, u32[]{:S(2)}, u32[]{:S(2)}) collective-permute-start(f32[4,2,32,256]{3,2,1,0:T(8,128)S(1)} %get-tuple-element.70), channel_id=1, source_target_pairs={{0,8},{8,0},{16,24},{24,16},{1,9},{9,1},{17,25},{25,17},{2,10},{10... | collective-permute-start | bytes 786440 | tf_op jit(solution)/shard_map/ppermute | solution.py:420
  34.6 18.7 %collective-permute-start.13 = (f32[4,1,32,256]{3,2,0,1:T(8,128)S(1)}, f32[4,1,32,256]{3,2,0,1:T(8,128)S(1)}, u32[]{:S(2)}, u32[]{:S(2)}) collective-permute-start(f32[4,1,32,256]{3,2,0,1:T(8,128)S(1)} %bitcast.13), channel_id=1, source_target_pairs={{0,16},{8,24},{16,0},{24,8},{1,17},{9,25},{17,1},{25,9},{2,18},{10... | collective-permute-start | bytes 393224 | tf_op jit(solution)/shard_map/ppermute | solution.py:420
  41.9 12.9 %collective-permute-start.18 = (f32[4,1,32,256]{3,2,0,1:T(8,128)S(1)}, f32[4,1,32,256]{3,2,0,1:T(8,128)S(1)}, u32[]{:S(2)}, u32[]{:S(2)}) collective-permute-start(f32[4,1,32,256]{3,2,0,1:T(8,128)S(1)} %bitcast.14), channel_id=1, source_target_pairs={{0,16},{8,24},{16,0},{24,8},{1,17},{9,25},{17,1},{25,9},{2,18},{10... | collective-permute-start | bytes 393224 | tf_op jit(solution)/shard_map/ppermute | solution.py:420
  43.1 5.5 %collective-permute-start.1 = (f32[4,2,8,256]{3,2,1,0:T(8,128)S(1)}, f32[4,2,8,256]{3,2,1,0:T(8,128)S(1)}, u32[]{:S(2)}, u32[]{:S(2)}) collective-permute-start(f32[4,2,8,256]{3,2,1,0:T(8,128)S(1)} %get-tuple-element.43), channel_id=1, source_target_pairs={{0,2},{2,4},{4,6},{6,0},{1,3},{3,5},{5,7},{7,1},{8,10},{10,12},{12... | collective-permute-start | bytes 196616 | tf_op jit(solution)/shard_map/ppermute | solution.py:415
  43.9 6.4 %collective-permute-start.2 = (f32[4,2,8,256]{3,2,1,0:T(8,128)S(1)}, f32[4,2,8,256]{3,2,1,0:T(8,128)S(1)}, u32[]{:S(2)}, u32[]{:S(2)}) collective-permute-start(f32[4,2,8,256]{3,2,1,0:T(8,128)S(1)} %get-tuple-element.44), channel_id=1, source_target_pairs={{0,6},{2,0},{4,2},{6,4},{1,7},{3,1},{5,3},{7,5},{8,14},{10,8},{12,... | collective-permute-start | bytes 196616 | tf_op jit(solution)/shard_map/ppermute | solution.py:415
  46.1 7.1 %collective-permute-start.6 = (f32[4,16,256]{2,1,0:T(8,128)S(1)}, f32[4,16,256]{2,1,0:T(8,128)S(1)}, u32[]{:S(2)}, u32[]{:S(2)}) collective-permute-start(f32[4,16,256]{2,1,0:T(8,128)S(1)} %get-tuple-element.50), channel_id=1, source_target_pairs={{0,8},{8,0},{16,24},{24,16},{1,9},{9,1},{17,25},{25,17},{2,10},{10... | collective-permute-start | bytes 196616 | tf_op jit(solution)/shard_map/ppermute | solution.py:420
  48.6 10.4 %collective-permute-start.7 = (f32[4,16,256]{2,1,0:T(8,128)S(1)}, f32[4,16,256]{2,1,0:T(8,128)S(1)}, u32[]{:S(2)}, u32[]{:S(2)}) collective-permute-start(f32[4,16,256]{2,1,0:T(8,128)S(1)} %get-tuple-element.51), channel_id=1, source_target_pairs={{0,16},{8,24},{16,0},{24,8},{1,17},{9,25},{17,1},{25,9},{2,18},{10... | collective-permute-start | bytes 196616 | tf_op jit(solution)/shard_map/ppermute | solution.py:420
  50.2 8.8 %collective-permute-start.8 = (f32[4,16,256]{2,1,0:T(8,128)S(1)}, f32[4,16,256]{2,1,0:T(8,128)S(1)}, u32[]{:S(2)}, u32[]{:S(2)}) collective-permute-start(f32[4,16,256]{2,1,0:T(8,128)S(1)} %get-tuple-element.52), channel_id=1, source_target_pairs={{0,24},{8,16},{16,8},{24,0},{1,25},{9,17},{17,9},{25,1},{2,26},{10... | collective-permute-start | bytes 196616 | tf_op jit(solution)/shard_map/ppermute | solution.py:420
  53.2 5.9 %collective-permute-start.3 = (f32[4,16,256]{2,1,0:T(8,128)S(1)}, f32[4,16,256]{2,1,0:T(8,128)S(1)}, u32[]{:S(2)}, u32[]{:S(2)}) collective-permute-start(f32[4,16,256]{2,1,0:T(8,128)S(1)} %get-tuple-element.46), channel_id=1, source_target_pairs={{0,8},{8,0},{16,24},{24,16},{1,9},{9,1},{17,25},{25,17},{2,10},{10... | collective-permute-start | bytes 196616 | tf_op jit(solution)/shard_map/ppermute | solution.py:420
  53.3 8.0 %collective-permute-start.4 = (f32[4,16,256]{2,1,0:T(8,128)S(1)}, f32[4,16,256]{2,1,0:T(8,128)S(1)}, u32[]{:S(2)}, u32[]{:S(2)}) collective-permute-start(f32[4,16,256]{2,1,0:T(8,128)S(1)} %get-tuple-element.47), channel_id=1, source_target_pairs={{0,16},{8,24},{16,0},{24,8},{1,17},{9,25},{17,1},{25,9},{2,18},{10... | collective-permute-start | bytes 196616 | tf_op jit(solution)/shard_map/ppermute | solution.py:420
  54.8 6.5 %collective-permute-start.5 = (f32[4,16,256]{2,1,0:T(8,128)S(1)}, f32[4,16,256]{2,1,0:T(8,128)S(1)}, u32[]{:S(2)}, u32[]{:S(2)}) collective-permute-start(f32[4,16,256]{2,1,0:T(8,128)S(1)} %get-tuple-element.48), channel_id=1, source_target_pairs={{0,24},{8,16},{16,8},{24,0},{1,25},{9,17},{17,9},{25,1},{2,26},{10... | collective-permute-start | bytes 196616 | tf_op jit(solution)/shard_map/ppermute | solution.py:420
